TPU v7x, 32 devices: a whole 2x2x4 slice. The times are simulated.
32 devices in a mesh: strip: 2 (over x), swath: 8 (over z, y), group: 2 (over core).
Axes of the slice: x: 2, y: 2, z: 4, core: 2. Of those that a mesh axis runs over, the one named last changes fastest.
Arguments:
- tokens_b: bfloat16 [256, 256, 384], P(('strip', 'swath'), 'group'), parts along dimension 0
- tokens_a: bfloat16 [256, 256, 384], P(('strip', 'swath'), 'group'), parts along dimension 0
- pack_rows: int32 [16, 2, 16, 1024], P(('strip', 'swath'), 'group'), parts along dimension 0, may hold values from 0 to 2047, as said below
- pack_count: int32 [16, 2, 16], P(('strip', 'swath'), 'group'), parts along dimension 0, may hold values from 0 to 1024, as said below
- gather_slots: int32 [4, 256, 256], P(None, ('strip', 'swath'), 'group'), parts along dimension 1, may hold values from 0 to 16383, as said below
- blend_weights: float32 [4, 256, 256], P(None, ('strip', 'swath'), 'group'), parts along dimension 1, may hold values from 0 to 1
- swath_gain: float32 [384], replicated, may hold values from 0.5 to 1.5
- swath_query: bfloat16 [384, 384], replicated
- swath_key: bfloat16 [384, 384], replicated
- swath_value: bfloat16 [384, 384], replicated, may hold values from -0.3125 to 0.3125
- swath_out: bfloat16 [384, 384], replicated, may hold values from -0.3125 to 0.3125
- query_gain: float32 [384], replicated, may hold values from 0.5 to 1.5
- source_gain: float32 [384], replicated, may hold values from 0.5 to 1.5
- cross_query: bfloat16 [384, 384], replicated
- cross_key: bfloat16 [384, 384], replicated
- cross_value: bfloat16 [384, 384], replicated, may hold values from -0.3125 to 0.3125
- cross_out: bfloat16 [384, 384], replicated, may hold values from -0.3125 to 0.3125
- conv_gain: float32 [384], replicated, may hold values from 0.5 to 1.5
- conv_first: bfloat16 [3, 3, 384, 384], replicated, may hold values from -0.109375 to 0.109375
- conv_second: bfloat16 [3, 3, 384, 384], replicated, may hold values from -0.109375 to 0.109375
Outputs:
- merged: bfloat16 [256, 256, 384], P(('strip', 'swath'), 'group'), parts along dimension 0
There are 2 independent parts, one for each index of `strip`. A program takes and returns all parts, laid end to end along the dimension named above; an argument that names none is the same for every part. Nothing has to cross between parts.
Inputs may be any that keep to these rules, and one draw needn't show every extreme that they name: `pack_rows`: entry [s, g, e, c] is a cell of device (s, g)'s block; the first pack_count[s, g, e] entries of a block are distinct. `pack_count`: zero unless the destination device's swath index differs from the source's by at most one; every destination receives exactly 1024 live rows from one of its sources. `gather_slots`: entry [k, i, j] is p * 1024 + c with p a source device whose swath index differs from that of the device holding cell (i, j) by at most one.
All inputs are finite; a program needn't handle non-finite values.
Results may differ from a plain program's by a relative error of at most 0.0095.
Values may be sent and summed in bfloat16 or wider, within the bound.
No kernel may reach another device: no remote copies, remote signals or barrier semaphores. Data moves between devices by JAX's collectives and lax.ppermute only.
A program may use at most 128 MiB of HBM per device.

v0:
```python
import math

import jax
import jax.numpy as jnp
from jax import lax
from jax.sharding import PartitionSpec as P

HEADS = 6
HD = 64
TILE_R = 16
TILE_C = 16


EPSILON = 1e-06


def shifted_2(array, axis, by):
    size = lax.axis_size(axis)
    pairs = [(i, i + by) for i in range(size) if 0 <= i + by < size]
    return lax.ppermute(array, axis, pairs)


def extended(block, sides, width):
    for axis, dim in sides:
        count = lax.axis_size(axis)
        forward = [(i, i + 1) for i in range(count - 1)]
        backward = [(target, source) for source, target in forward]
        low = lax.ppermute(
            lax.slice_in_dim(block, block.shape[dim] - width, None, axis=dim), axis, forward
        )
        high = lax.ppermute(lax.slice_in_dim(block, 0, width, axis=dim), axis, backward)
        block = jnp.concatenate([low, block, high], axis=dim)
    return block


def rms_gain(values, gain_vector):
    widened = values.astype(jnp.float32)
    inverse = lax.rsqrt(jnp.mean(widened * widened, axis=-1, keepdims=True) + EPSILON)
    return (widened * inverse * gain_vector).astype(jnp.bfloat16)


def project(values, matrix):
    flattened = values.reshape(-1, values.shape[-1])
    result = jnp.dot(flattened, matrix, preferred_element_type=jnp.float32)
    return result.reshape(values.shape[:-1] + (matrix.shape[-1],))


def window_mask(height, breadth, margin):
    row_place = lax.axis_index("swath") * height - margin + jnp.arange(height + 2 * margin)
    col_place = lax.axis_index("group") * breadth - margin + jnp.arange(breadth + 2 * margin)
    row_live = (row_place >= 0) & (row_place < height * lax.axis_size("swath"))
    col_live = (col_place >= 0) & (col_place < breadth * lax.axis_size("group"))
    return row_live[:, None] & col_live[None, :]


def split_blocks(field, block_rows, block_cols):
    height, breadth, channels = field.shape
    shaped = field.reshape(
        height // block_rows, block_rows, breadth // block_cols, block_cols, channels
    )
    return shaped.transpose(0, 2, 1, 3, 4).reshape(-1, block_rows * block_cols, channels)


def join_blocks(blocks, height, breadth, block_rows, block_cols):
    channels = blocks.shape[-1]
    shaped = blocks.reshape(
        height // block_rows, breadth // block_cols, block_rows, block_cols, channels
    )
    return shaped.transpose(0, 2, 1, 3, 4).reshape(height, breadth, channels)


def window_attend(query_field, key_field, value_field, live_mask):
    height, breadth, channels = query_field.shape
    block_rows = math.gcd(height, 8)
    block_cols = math.gcd(breadth, 8)
    block_span = breadth // block_cols
    block_total = height // block_rows * block_span
    length = block_rows * block_cols
    ext_rows = block_rows + 6
    ext_cols = block_cols + 6
    extent = ext_rows * ext_cols
    batch_blocks = math.gcd(block_total, 32)
    group_total = block_total // batch_blocks
    local_row = jnp.arange(length, dtype=jnp.int32) // block_cols
    local_col = jnp.arange(length, dtype=jnp.int32) % block_cols
    key_row = jnp.arange(extent, dtype=jnp.int32) // ext_cols
    key_col = jnp.arange(extent, dtype=jnp.int32) % ext_cols
    row_gap = key_row[None, :] - local_row[:, None]
    col_gap = key_col[None, :] - local_col[:, None]
    inside = (row_gap >= 0) & (row_gap <= 6) & (col_gap >= 0) & (col_gap <= 6)
    block_ids = jnp.arange(block_total, dtype=jnp.int32)
    row_starts = (block_ids // block_span * block_rows).reshape(group_total, batch_blocks)
    col_starts = (block_ids % block_span * block_cols).reshape(group_total, batch_blocks)
    query_groups = split_blocks(query_field, block_rows, block_cols).reshape(
        group_total, batch_blocks, length, HEADS, HD
    )
    score_scale = HD ** (-0.5)

    def one_block(row_start, col_start):
        zero = jnp.zeros((), jnp.int32)
        key_block = lax.dynamic_slice(
            key_field, (row_start, col_start, zero), (ext_rows, ext_cols, channels)
        )
        value_block = lax.dynamic_slice(
            value_field, (row_start, col_start, zero), (ext_rows, ext_cols, channels)
        )
        live_block = lax.dynamic_slice(live_mask, (row_start, col_start), (ext_rows, ext_cols))
        return (
            key_block.reshape(extent, HEADS, HD),
            value_block.reshape(extent, HEADS, HD),
            live_block.reshape(extent),
        )

    def attend_group(operands):
        query_blocks, row_group, col_group = operands
        key_blocks, value_blocks, live_blocks = jax.vmap(one_block)(row_group, col_group)
        scores = (
            jnp.einsum(
                "tlhd,tmhd->thlm", query_blocks, key_blocks, preferred_element_type=jnp.float32
            )
            * score_scale
        )
        allowed = inside[None, None, :, :] & live_blocks[:, None, None, :]
        scores = jnp.where(allowed, scores, -jnp.inf)
        row_peak = jnp.max(scores, axis=-1, keepdims=True)
        raised = jnp.exp(scores - row_peak)
        attn_weights = (raised / jnp.sum(raised, axis=-1, keepdims=True)).astype(jnp.bfloat16)
        mixed = jnp.einsum(
            "thlm,tmhd->tlhd", attn_weights, value_blocks, preferred_element_type=jnp.float32
        )
        return mixed.astype(jnp.bfloat16)

    mixed_groups = lax.map(attend_group, (query_groups, row_starts, col_starts))
    return join_blocks(
        mixed_groups.reshape(block_total, length, channels), height, breadth, block_rows, block_cols
    )


def resample(shifted, pack_rows, pack_count, gather_slots, blend_weights):
    height, breadth, channels = shifted.shape
    flattened = shifted.reshape(height * breadth, channels)
    cap_slots = pack_rows.shape[-1]
    peer_total = pack_rows.shape[-2]
    row_table = pack_rows.reshape(peer_total, cap_slots)
    count_table = pack_count.reshape(peer_total)
    slot_iota = jnp.arange(cap_slots)
    group_total = lax.axis_size("group")
    swath_here = lax.axis_index("swath")
    swath_last = lax.axis_size("swath") - 1

    def packed(row_part, count_part):
        picked = jnp.take(flattened, row_part.reshape(-1), axis=0).reshape(
            row_part.shape + (channels,)
        )
        keep = slot_iota[None, :] < count_part[:, None]
        return jnp.where(keep[:, :, None], picked, jnp.zeros_like(picked))

    def block_for(step_by):
        target = jnp.clip(swath_here + step_by, 0, swath_last) * group_total
        return packed(
            lax.dynamic_slice_in_dim(row_table, target, group_total, 0),
            lax.dynamic_slice_in_dim(count_table, target, group_total, 0),
        )

    received = []
    stacked = jnp.stack([block_for(1), block_for(0), block_for(-1)], axis=0)
    stacked = lax.all_to_all(stacked, "group", split_axis=1, concat_axis=1, tiled=True)
    for layer, step_by in enumerate((1, 0, -1)):
        block = stacked[layer]
        if step_by != 0:
            block = shifted_2(block, "swath", step_by)
        received.append(block)
    table = jnp.concatenate(received, axis=0).reshape(-1, channels)
    source_peer = gather_slots // cap_slots
    source_rel = jnp.clip(source_peer // group_total - swath_here + 1, 0, 2)
    slot_index = (
        source_rel * group_total + source_peer % group_total
    ) * cap_slots + gather_slots % cap_slots
    accumulated = jnp.zeros((height, breadth, channels), jnp.float32)
    for ref_step in range(4):
        picked = jnp.take(table, slot_index[ref_step].reshape(-1), axis=0).reshape(
            height, breadth, channels
        )
        accumulated = accumulated + blend_weights[ref_step][:, :, None] * picked.astype(jnp.float32)
    return accumulated.astype(jnp.bfloat16)


def tile_attend(query_field, key_field, value_field):
    height, breadth, channels = query_field.shape
    length = TILE_R * TILE_C
    query_tiles = split_blocks(query_field, TILE_R, TILE_C).reshape(-1, length, HEADS, HD)
    key_tiles = split_blocks(key_field, TILE_R, TILE_C).reshape(-1, length, HEADS, HD)
    value_tiles = split_blocks(value_field, TILE_R, TILE_C).reshape(-1, length, HEADS, HD)
    scores = jnp.einsum(
        "tlhd,tmhd->thlm", query_tiles, key_tiles, preferred_element_type=jnp.float32
    ) * HD ** (-0.5)
    row_peak = jnp.max(scores, axis=-1, keepdims=True)
    raised = jnp.exp(scores - row_peak)
    attn_weights = (raised / jnp.sum(raised, axis=-1, keepdims=True)).astype(jnp.bfloat16)
    tile_mix = jnp.einsum(
        "thlm,tmhd->tlhd", attn_weights, value_tiles, preferred_element_type=jnp.float32
    ).astype(jnp.bfloat16)
    return join_blocks(tile_mix.reshape(-1, length, channels), height, breadth, TILE_R, TILE_C)


def conv_valid(padded, kernel):
    height = padded.shape[0] - 2
    breadth = padded.shape[1] - 2
    accumulated = jnp.zeros((height, breadth, kernel.shape[-1]), jnp.float32)
    for row_step in range(3):
        for col_step in range(3):
            accumulated = accumulated + project(
                padded[row_step : row_step + height, col_step : col_step + breadth],
                kernel[row_step, col_step],
            )
    return accumulated


def body(
    tokens_b,
    tokens_a,
    pack_rows,
    pack_count,
    gather_slots,
    blend_weights,
    swath_gain,
    swath_query,
    swath_key,
    swath_value,
    swath_out,
    query_gain,
    source_gain,
    cross_query,
    cross_key,
    cross_value,
    cross_out,
    conv_gain,
    conv_first,
    conv_second,
):
    height, breadth, channels = tokens_b.shape
    normed = rms_gain(tokens_b, swath_gain)
    query_field = project(normed, swath_query).astype(jnp.bfloat16)
    key_value = jnp.concatenate(
        [
            project(normed, swath_key).astype(jnp.bfloat16),
            project(normed, swath_value).astype(jnp.bfloat16),
        ],
        axis=-1,
    )
    widened = extended(key_value, (("swath", 0), ("group", 1)), 3)
    key_field = widened[:, :, :channels]
    value_field = widened[:, :, channels:]
    window_mix = window_attend(query_field, key_field, value_field, window_mask(height, breadth, 3))
    shifted = (tokens_b.astype(jnp.float32) + project(window_mix, swath_out)).astype(jnp.bfloat16)
    resampled = resample(shifted, pack_rows, pack_count, gather_slots, blend_weights)
    normed_a = rms_gain(tokens_a, query_gain)
    normed_r = rms_gain(resampled, source_gain)
    query_a = project(normed_a, cross_query).astype(jnp.bfloat16)
    key_r = project(normed_r, cross_key).astype(jnp.bfloat16)
    value_r = project(normed_r, cross_value).astype(jnp.bfloat16)
    tile_mix = tile_attend(query_a, key_r, value_r)
    joined = (tokens_a.astype(jnp.float32) + project(tile_mix, cross_out)).astype(jnp.bfloat16)
    normed_c = rms_gain(joined, conv_gain)
    padded_c = extended(normed_c, (("swath", 0), ("group", 1)), 1)
    inner_field = jax.nn.gelu(conv_valid(padded_c, conv_first), approximate=True).astype(
        jnp.bfloat16
    )
    padded_inner = extended(inner_field, (("swath", 0), ("group", 1)), 1)
    second = conv_valid(padded_inner, conv_second)
    return (joined.astype(jnp.float32) + second).astype(jnp.bfloat16)


def solution(mesh):
    placed = (
        P(("strip", "swath"), "group", None),
        P(("strip", "swath"), "group", None),
        P(("strip", "swath"), "group", None, None),
        P(("strip", "swath"), "group", None),
        P(None, ("strip", "swath"), "group"),
        P(None, ("strip", "swath"), "group"),
        P(),
        P(),
        P(),
        P(),
        P(),
        P(),
        P(),
        P(),
        P(),
        P(),
        P(),
        P(),
        P(),
        P(),
    )
    return jax.shard_map(
        body,
        mesh=mesh,
        in_specs=placed,
        out_specs=P(("strip", "swath"), "group", None),
        check_vma=False,
    )
```

profile of v0, /device:TPU:11, one launch (start us, length us, event | category | flops | bytes accessed | tf_op | source)
XLA Modules:
  0.0 694.8 jit_solution(1475857650569158056)
XLA Ops:
  7.0 3.1 collective-permute-start
  10.1 3.0 collective-permute-start.1
  17.3 5.9 squeeze.73
  23.3 63.3 %while.8 = (s32[]{:T(128)}, pred[22,134]{1,0:T(8,128)(4,1)S(1)}, s32[32,2]{0,1:T(2,128)S(1)}, pred[32,14,14]{2,1,0:T(8,128)(4,1)S(1)}, s32[]{:T(128)}) while((s32[]{:T(128)}, pred[22,134]{1,0:T(8,128)(4,1)S(1)}, s32[32,2]{0,1:T(2,128)S(1)}, pred[32,14,14]{2,1,0:T(8,128)(4,1)S(1)}, s32[]{:T(128)}) %tuple.88), condition=%wide.while_cond.1, body=%wide.while_body.1.sunk | while | flops 2 | bytes 4205 | solution.py:107
  91.4 3.4 collective-permute-start.3
  95.5 4.3 pad_maximum_fusion.2
  104.5 117.0 %while.9 = (s32[]{:T(128)}, bf16[22,134,384]{2,1,0:T(8,128)(2,1)}, s32[32,3]{0,1:T(4,128)S(1)}, bf16[32,14,14,384]{3,2,1,0:T(8,128)(2,1)}, s32[]{:T(128)}) while((s32[]{:T(128)}, bf16[22,134,384]{2,1,0:T(8,128)(2,1)}, s32[32,3]{0,1:T(4,128)S(1)}, bf16[32,14,14,384]{3,2,1,0:T(8,128)(2,1)}, s32[]{:T(128)}) %tuple.85), condition=%wide.while_cond.2, body=%wide.while_body.2.sunk | while | flops 2 | bytes 345705 | solution.py:101
  105.2 3.0 bitcast_dynamic-update-slice_fusion.8
  108.9 3.0 bitcast_dynamic-update-slice_fusion.8
  116.2 3.0 bitcast_dynamic-update-slice_fusion.8
  119.8 3.0 bitcast_dynamic-update-slice_fusion.8
  130.8 3.0 bitcast_dynamic-update-slice_fusion.8
  134.4 3.0 bitcast_dynamic-update-slice_fusion.8
  141.7 3.0 bitcast_dynamic-update-slice_fusion.8
  145.4 3.0 bitcast_dynamic-update-slice_fusion.8
  149.1 3.0 bitcast_dynamic-update-slice_fusion.8
  152.7 3.0 bitcast_dynamic-update-slice_fusion.8
  156.4 3.0 bitcast_dynamic-update-slice_fusion.8
  163.7 3.0 bitcast_dynamic-update-slice_fusion.8
  171.0 3.0 bitcast_dynamic-update-slice_fusion.8
  174.7 3.0 bitcast_dynamic-update-slice_fusion.8
  178.3 3.0 bitcast_dynamic-update-slice_fusion.8
  185.7 3.0 bitcast_dynamic-update-slice_fusion.8
  189.3 3.0 bitcast_dynamic-update-slice_fusion.8
  196.6 3.0 bitcast_dynamic-update-slice_fusion.8
  200.3 3.0 bitcast_dynamic-update-slice_fusion.8
  203.9 3.0 bitcast_dynamic-update-slice_fusion.8
  207.6 3.0 bitcast_dynamic-update-slice_fusion.8
  214.9 3.0 bitcast_dynamic-update-slice_fusion.8
  221.6 16.1 %reshape.730 = bf16[32,196,6,64]{3,2,1,0:T(8,128)(2,1)} reshape(bf16[32,14,14,384]{3,2,1,0:T(8,128)(2,1)} %get-tuple-element.57) | data formatting | bytes 9633792 | tf_op jit(solution)/shard_map/while/body/eval_jaxpr/vmap()/reshape | solution.py:109
  240.6 86.2 %while.3 = (s32[]{:T(128)}, bf16[22,134,384]{2,1,0:T(8,128)(2,1)S(1)}, s32[32,3]{0,1:T(4,128)S(1)}, bf16[32,14,14,384]{3,2,1,0:T(8,128)(2,1)}, s32[]{:T(128)}) while((s32[]{:T(128)}, bf16[22,134,384]{2,1,0:T(8,128)(2,1)S(1)}, s32[32,3]{0,1:T(4,128)S(1)}, bf16[32,14,14,384]{3,2,1,0:T(8,128)(2,1)}, s32[]{:T(128)}) %tuple.94), condition=%wide.while_cond, body=%wide.while_body.sunk | while | flops 2 | bytes 324201 | solution.py:104
  326.8 16.1 %reshape.728 = bf16[32,196,6,64]{3,2,1,0:T(8,128)(2,1)} reshape(bf16[32,14,14,384]{3,2,1,0:T(8,128)(2,1)} %get-tuple-element.41) | data formatting | bytes 9633792 | tf_op jit(solution)/shard_map/while/body/eval_jaxpr/vmap()/reshape | solution.py:110
  343.0 16.9 %fusion.3 = f32[32,6,64,196]{3,2,1,0:T(8,128)} fusion(bf16[32,196,6,64]{3,2,1,0:T(8,128)(2,1)} %reshape.730, bf16[32,64,6,64]{3,2,1,0:T(8,128)(2,1)} %squeeze.73), kind=kOutput, calls=%fused_computation.22 | convolution fusion | flops 308281344 | bytes 16023552 | tf_op jit(solution)/shard_map/while/body/eval_jaxpr/tlhd,tmhd->thlm/dot_general | solution.py:118
  359.9 15.9 %fusion.190 = (f32[32,6,64]{2,1,0:T(8,128)S(1)}, f32[32,6,64,196]{3,2,1,0:T(8,128)}) fusion(f32[32,6,64,196]{3,2,1,0:T(8,128)} %fusion.3, pred[32,64,196]{2,1,0:T(8,128)(4,1)S(1)} %copy-done.8), kind=kOutput, calls=%fused_computation.319 | output fusion | flops 14450883 | bytes 19718144 | tf_op jit(solution)/shard_map/while/body/eval_jaxpr/sub | solution.py:126
  375.8 11.2 %convert_bitcast_fusion = bf16[32,64,6,64]{1,3,2,0:T(8,128)(2,1)S(1)} fusion(f32[32,6,64,196]{3,2,1,0:T(8,128)} %get-tuple-element.130, f32[32,6,64]{2,1,0:T(8,128)S(1)} %get-tuple-element.129, bf16[32,196,6,64]{3,2,1,0:T(8,128)(2,1)} %reshape.728), kind=kOutput, calls=%fused_computation.76 | convolution fusion | flops 313884672 | bytes 16072704 | tf_op jit(solution)/shard_map/while/body/eval_jaxpr/thlm,tmhd->tlhd/dot_general | solution.py:128
  387.0 5.2 copy.73
  392.2 5.3 reshape_reshape.18
  399.6 9.1 %gather_fusion.1 = bf16[2048,384]{1,0:T(8,128)(2,1)} fusion(bf16[2048,384]{1,0:T(8,128)(2,1)S(1)} %bitcast.276, s32[2048]{0:T(1024)S(1)} %get-tuple-element.144), kind=kCustom, calls=%fused_computation.2.clone | custom fusion | bytes 3153920 | tf_op jit(solution)/shard_map/jit(_take)/gather | solution.py:152
  408.7 9.1 %gather_fusion = bf16[2048,384]{1,0:T(8,128)(2,1)} fusion(bf16[2048,384]{1,0:T(8,128)(2,1)S(1)} %bitcast.277, s32[2048]{0:T(1024)S(1)} %get-tuple-element.143), kind=kCustom, calls=%fused_computation.clone | custom fusion | bytes 3153920 | tf_op jit(solution)/shard_map/jit(_take)/gather | solution.py:152
  417.7 7.5 %gather_fusion.2 = bf16[2048,384]{1,0:T(8,128)(2,1)S(1)} fusion(bf16[2048,384]{1,0:T(8,128)(2,1)S(1)} %bitcast.278, s32[2048]{0:T(1024)S(1)} %fusion.165), kind=kCustom, calls=%fused_computation.3.clone | custom fusion | bytes 3153920 | tf_op jit(solution)/shard_map/jit(_take)/gather | solution.py:152
  430.0 7.5 %all_to_all.5 = bf16[3,2,1024,384]{3,2,0,1:T(8,128)(2,1)S(1)} all-to-all(bf16[3,2,1024,384]{3,2,0,1:T(8,128)(2,1)S(1)} %pad_maximum_fusion), channel_id=1, replica_groups=mesh['strip'=2,'swath'=8,'group'=2] {'group'}, dimensions={1} | all-to-all | bytes 9437184 | tf_op jit(solution)/shard_map/all_to_all | solution.py:167
  441.9 4.0 collective-permute-start.5
  447.7 4.2 reshape_reshape.20
  452.0 57.3 %collective-permute-done.4 = bf16[2,1024,384]{2,1,0:T(8,128)(2,1)} collective-permute-done((bf16[2,1024,384]{2,1,0:T(8,128)(2,1)}, bf16[2,1024,384]{2,1,0:T(8,128)(2,1)}, u32[]{:S(2)}, u32[]{:S(2)}) %collective-permute-start.4) | collective-permute-done | bytes 1572896 | tf_op jit(solution)/shard_map/ppermute | solution.py:20
  509.3 3.5 collective-permute-done.5
  512.8 3.8 pad_maximum_fusion.1
  516.6 10.1 %gather_fusion.3 = bf16[2048,384]{1,0:T(8,128)(2,1)S(1)} fusion(bf16[6144,384]{1,0:T(8,128)(2,1)} %bitcast.279, s32[2048]{0:T(1024)S(1)} %get-tuple-element.122), kind=kCustom, calls=%fused_computation.1.clone | custom fusion | bytes 3153920 | tf_op jit(solution)/shard_map/jit(_take)/gather | solution.py:181
  526.8 10.1 %gather_fusion.4 = bf16[2048,384]{1,0:T(8,128)(2,1)S(1)} fusion(bf16[6144,384]{1,0:T(8,128)(2,1)} %bitcast.280, s32[2048]{0:T(1024)S(1)} %get-tuple-element.125), kind=kCustom, calls=%fused_computation.4.clone | custom fusion | bytes 3153920 | tf_op jit(solution)/shard_map/jit(_take)/gather | solution.py:181
  536.9 11.8 %gather_fusion.5 = bf16[2048,384]{1,0:T(8,128)(2,1)} fusion(bf16[6144,384]{1,0:T(8,128)(2,1)} %bitcast.281, s32[2048]{0:T(1024)S(1)} %get-tuple-element.124), kind=kCustom, calls=%fused_computation.5.clone | custom fusion | bytes 3153920 | tf_op jit(solution)/shard_map/jit(_take)/gather | solution.py:181
  548.8 11.8 %gather_fusion.6 = bf16[2048,384]{1,0:T(8,128)(2,1)} fusion(bf16[6144,384]{1,0:T(8,128)(2,1)} %bitcast.282, s32[2048]{0:T(1024)S(1)} %get-tuple-element.123), kind=kCustom, calls=%fused_computation.6.clone | custom fusion | bytes 3153920 | tf_op jit(solution)/shard_map/jit(_take)/gather | solution.py:181
  560.6 6.5 fusion.15
  569.4 3.9 reshape_reshape.21
  573.3 9.8 %fusion.39 = f32[8,6,256,256]{2,3,1,0:T(8,128)} fusion(bf16[8,256,6,64]{3,2,1,0:T(8,128)(2,1)} %reshape_reshape.21, bf16[8,256,6,64]{3,2,1,0:T(8,128)(2,1)} %reshape_reshape.20), kind=kOutput, calls=%fused_computation.71 | convolution fusion | flops 402653184 | bytes 15728640 | tf_op jit(solution)/shard_map/tlhd,tmhd->thlm/dot_general | solution.py:194
  583.1 15.9 %fusion.191 = (f32[8,6,256]{2,1,0:T(8,128)S(1)}, f32[8,6,256,256]{2,3,1,0:T(8,128)}) fusion(f32[8,6,256,256]{2,3,1,0:T(8,128)} %fusion.39), kind=kOutput, calls=%fused_computation.320 | output fusion | flops 12583167 | bytes 25214976 | tf_op jit(solution)/shard_map/sub | solution.py:198
  600.2 3.7 reshape_reshape.19
  603.9 7.3 %fusion.95 = bf16[8,256,6,64]{1,3,2,0:T(8,128)(2,1)S(1)} fusion(f32[8,6,256,256]{2,3,1,0:T(8,128)} %get-tuple-element.132, f32[8,6,256]{2,1,0:T(8,128)S(1)} %get-tuple-element.131, bf16[8,256,6,64]{3,2,1,0:T(8,128)(2,1)} %reshape_reshape.19), kind=kOutput, calls=%fused_computation.143 | convolution fusion | flops 409731072 | bytes 15777792 | tf_op jit(solution)/shard_map/thlm,tmhd->tlhd/dot_general | solution.py:200
  611.3 3.6 copy.87
  614.8 5.2 reshape_reshape.22
  625.5 4.5 collective-permute-start.7
  633.8 3.1 collective-permute-start.9
  651.7 5.8 fusion.37
  657.6 4.3 collective-permute-start.10
  670.1 3.0 collective-permute-start.13
  688.0 6.4 fusion.29
  (408 shorter events, 288.2 us)
Async XLA Ops:
  0.0 620.3 %copy-start = (bf16[384,384]{1,0:T(8,128)(2,1)S(1)}, bf16[384,384]{1,0:T(8,128)(2,1)}, u32[]{:S(2)}) copy-start(bf16[384,384]{1,0:T(8,128)(2,1)} %param.40) | copy-start | bytes 884740
  0.0 4.6 copy-start.1
  0.0 4.6 copy-start.19
  0.0 4.6 copy-start.17
  7.0 82.2 %collective-permute-start = (bf16[3,128,768]{2,1,0:T(8,128)(2,1)}, bf16[3,128,768]{2,1,0:T(8,128)(2,1)}, u32[]{:S(2)}, u32[]{:S(2)}) collective-permute-start(bf16[3,128,768]{2,1,0:T(8,128)(2,1)} %get-tuple-element.97), channel_id=1, source_target_pairs={{0,2},{2,4},{4,6},{6,8},{8,10},{10,12},{12,14},{1,3},{3,5},{5,7},{... | collective-permute-start | bytes 1769480 | tf_op jit(solution)/shard_map/ppermute | solution.py:28
  10.1 79.0 %collective-permute-start.1 = (bf16[3,128,768]{2,1,0:T(8,128)(2,1)}, bf16[3,128,768]{2,1,0:T(8,128)(2,1)}, u32[]{:S(2)}, u32[]{:S(2)}) collective-permute-start(bf16[3,128,768]{2,1,0:T(8,128)(2,1)} %get-tuple-element.98), channel_id=1, source_target_pairs={{2,0},{4,2},{6,4},{8,6},{10,8},{12,10},{14,12},{3,1},{5,3},{7,5},{... | collective-permute-start | bytes 1769480 | tf_op jit(solution)/shard_map/ppermute | solution.py:31
  17.3 70.4 %copy-start.14 = (s32[1,1,16]{2,1,0:T(1,128)S(1)}, s32[1,1,16]{2,1,0:T(1,128)}, u32[]{:S(2)}) copy-start(s32[1,1,16]{2,1,0:T(1,128)} %param.27) | copy-start | bytes 196
  90.1 4.7 collective-permute-start.2
  91.4 4.1 collective-permute-start.3
  342.9 16.9 %copy-start.8 = (pred[32,64,196]{2,1,0:T(8,128)(4,1)S(1)}, pred[32,64,196]{2,1,0:T(8,128)(4,1)}, u32[]{:S(2)}) copy-start(pred[32,64,196]{2,1,0:T(8,128)(4,1)} %broadcast_and_fusion) | copy-start | bytes 1204228
  392.2 5.5 copy-start.2
  397.5 1.0 copy-start.9
  425.2 2.2 copy-start.3
  437.5 8.4 %copy-start.6 = (bf16[16,128,384]{2,1,0:T(8,128)(2,1)S(1)}, bf16[16,128,384]{2,1,0:T(8,128)(2,1)}, u32[]{:S(2)}) copy-start(bf16[16,128,384]{2,1,0:T(8,128)(2,1)} %param.25) | copy-start | bytes 4718596
  437.5 8.8 %copy-start.18 = (bf16[384,384]{1,0:T(8,128)(2,1)S(1)}, bf16[384,384]{1,0:T(8,128)(2,1)}, u32[]{:S(2)}) copy-start(bf16[384,384]{1,0:T(8,128)(2,1)} %param.37) | copy-start | bytes 884740
  437.5 8.8 %copy-start.20 = (f32[384]{0:T(512)S(1)}, f32[384]{0:T(512)}, u32[]{:S(2)}) copy-start(f32[384]{0:T(512)} %param.35) | copy-start | bytes 4612
  439.6 69.6 %collective-permute-start.4 = (bf16[2,1024,384]{2,1,0:T(8,128)(2,1)}, bf16[2,1024,384]{2,1,0:T(8,128)(2,1)}, u32[]{:S(2)}, u32[]{:S(2)}) collective-permute-start(bf16[2,1024,384]{2,1,0:T(8,128)(2,1)} %get-tuple-element.90), channel_id=1, source_target_pairs={{0,2},{2,4},{4,6},{6,8},{8,10},{10,12},{12,14},{1,3},{3,5},{5,7},{... | collective-permute-start | bytes 4718600 | tf_op jit(solution)/shard_map/ppermute | solution.py:20
  441.9 70.9 %collective-permute-start.5 = (bf16[2,1024,384]{2,1,0:T(8,128)(2,1)}, bf16[2,1024,384]{2,1,0:T(8,128)(2,1)}, u32[]{:S(2)}, u32[]{:S(2)}) collective-permute-start(bf16[2,1024,384]{2,1,0:T(8,128)(2,1)} %get-tuple-element.91), channel_id=1, source_target_pairs={{2,0},{4,2},{6,4},{8,6},{10,8},{12,10},{14,12},{3,1},{5,3},{7,5},{... | collective-permute-start | bytes 4718600 | tf_op jit(solution)/shard_map/ppermute | solution.py:20
  447.6 4.2 copy-start.12
  447.6 4.3 copy-start.13
  560.6 6.6 copy-start.15
  567.1 1.0 copy-start.10
  583.1 15.9 %copy-start.11 = (bf16[384,384]{1,0:T(8,128)(2,1)S(1)}, bf16[384,384]{1,0:T(8,128)(2,1)}, u32[]{:S(2)}) copy-start(bf16[384,384]{1,0:T(8,128)(2,1)} %param.39) | copy-start | bytes 884740
  620.0 1.4 copy-start.7
  620.3 2.6 copy-start.16
  622.9 7.1 %copy-start.4 = (bf16[3,3,384,384]{3,2,1,0:T(8,128)(2,1)S(1)}, bf16[3,3,384,384]{3,2,1,0:T(8,128)(2,1)}, u32[]{:S(2)}) copy-start(bf16[3,3,384,384]{3,2,1,0:T(8,128)(2,1)} %param.42) | copy-start | bytes 7962628
  623.4 7.7 %collective-permute-start.6 = (bf16[1,128,384]{2,1,0:T(8,128)(2,1)S(1)}, bf16[1,128,384]{2,1,0:T(8,128)(2,1)S(1)}, u32[]{:S(2)}, u32[]{:S(2)}) collective-permute-start(bf16[1,128,384]{2,1,0:T(8,128)(2,1)S(1)} %get-tuple-element.109), channel_id=1, source_target_pairs={{0,2},{2,4},{4,6},{6,8},{8,10},{10,12},{12,14},{1,3},{3,5},{5,7},{... | collective-permute-start | bytes 294920 | tf_op jit(solution)/shard_map/ppermute | solution.py:28
  625.5 7.0 %collective-permute-start.7 = (bf16[1,128,384]{2,1,0:T(8,128)(2,1)S(1)}, bf16[1,128,384]{2,1,0:T(8,128)(2,1)S(1)}, u32[]{:S(2)}, u32[]{:S(2)}) collective-permute-start(bf16[1,128,384]{2,1,0:T(8,128)(2,1)S(1)} %get-tuple-element.110), channel_id=1, source_target_pairs={{2,0},{4,2},{6,4},{8,6},{10,8},{12,10},{14,12},{3,1},{5,3},{7,5},{... | collective-permute-start | bytes 294920 | tf_op jit(solution)/shard_map/ppermute | solution.py:31
  632.5 6.7 collective-permute-start.8
  633.8 5.4 collective-permute-start.9
  657.6 8.9 %collective-permute-start.10 = (bf16[1,128,384]{2,1,0:T(8,128)(2,1)S(1)}, bf16[1,128,384]{2,1,0:T(8,128)(2,1)S(1)}, u32[]{:S(2)}, u32[]{:S(2)}) collective-permute-start(bf16[1,128,384]{2,1,0:T(8,128)(2,1)S(1)} %get-tuple-element.107), channel_id=1, source_target_pairs={{0,2},{2,4},{4,6},{6,8},{8,10},{10,12},{12,14},{1,3},{3,5},{5,7},{... | collective-permute-start | bytes 294920 | tf_op jit(solution)/shard_map/ppermute | solution.py:28
  661.9 11.2 %copy-start.5 = (bf16[3,3,384,384]{3,2,1,0:T(8,128)(2,1)S(1)}, bf16[3,3,384,384]{3,2,1,0:T(8,128)(2,1)}, u32[]{:S(2)}) copy-start(bf16[3,3,384,384]{3,2,1,0:T(8,128)(2,1)} %param.43) | copy-start | bytes 7962628
  661.9 6.8 collective-permute-start.11
  668.8 6.6 collective-permute-start.12
  670.1 5.3 collective-permute-start.13
where the time goes:
time: 705 us; the launch traced here: 695 us
  local copies, waits for them, and re-layouts  421 us (60%)
  matrix products  98.8 us (14%)
  waiting for transfers between devices  65.2 us (9%)
  other arithmetic  62 us (9%)
  starting transfers between devices  39 us (6%)
  blocking collectives  7.51 us (1%)
    gather x288, local copies, waits for them, and re-layouts  266 us
    ppermute x2, waiting for transfers between devices, shifted_2(): return lax.ppermute(array, axis, pairs)  60.8 us
    dot_general x26, matrix products, project(): result = jnp.dot(flattened, matrix, preferred_element_type=jnp.float32)  53.6 us
    gather x4, local copies, waits for them, and re-layouts, resample(): jnp.take(table, slot_index[ref_step].reshape(-1), axis=0)  44 us
    gather x3, local copies, waits for them, and re-layouts, packed(): jnp.take(flattened, row_part.reshape(-1), axis=0)  25.6 us
    ppermute x6, starting transfers between devices, extended(): lax.ppermute(lax.slice_in_dim(block, 0, width, axis=dim), axis, backward)  19.5 us
    dot_general x1, matrix products, attend_group(): jnp.einsum('tlhd,tmhd->thlm', query_blocks, key_blocks, preferred_element...  16.9 us
    reshape x1, local copies, waits for them, and re-layouts, one_block(): value_block.reshape(extent, HEADS, HD)  16.1 us
  transfers between devices with their start and end apart: 14, of which 5 were waited for; matrix products, arithmetic and copies ran while one was open for 13% of the time, Pallas kernels for 0%

commit v1 on v0

v1 whole, which is shorter than its diff:
```python
import functools

import jax
import jax.numpy as jnp
import numpy as np
from jax import lax
from jax.experimental import pallas as pl
from jax.experimental.pallas import tpu as pltpu
from jax.sharding import PartitionSpec as P


EPSILON = 1e-06
ROWS = 4
SPAN = ROWS + 6
QC = 16
KC = 24

def rms_rows(x, gain):
    inv = lax.rsqrt(jnp.mean(x * x, axis=-1, keepdims=True) + EPSILON)
    return x * inv * gain

def window_kernel(plan, place_ref, inside_ref, keyrow_ref, keycol_ref, gain_ref, wq_ref, wk_ref, wv_ref, wo_ref,
                  *rest):
    n_src = len(plan)
    srcs, edges = rest[:n_src], rest[n_src:2 * n_src]
    out_ref, tok, side, normed, qs, kv, mix, sems = rest[2 * n_src:]
    breadth = tok.shape[1]
    channels = tok.shape[2]
    wide = normed.shape[1]
    copies = []
    for n, (dst0, src0, count) in enumerate(plan):
        copies.append(pltpu.make_async_copy(srcs[n].at[pl.ds(src0, count)], tok.at[pl.ds(dst0, count)], sems.at[2 * n]))
        copies.append(pltpu.make_async_copy(edges[n].at[pl.ds(src0, count)], side.at[pl.ds(dst0, count)], sems.at[2 * n + 1]))
    for c in copies:
        c.start()
    gain = gain_ref[...]
    normed[:, breadth:, :] = jnp.zeros((SPAN, wide - breadth, channels), jnp.float32)
    for c in copies:
        c.wait()
    for r in range(SPAN):
        x = rms_rows(tok[r].astype(jnp.float32), gain)
        normed[r, 3:3 + breadth, :] = x
        if 3 <= r < 3 + ROWS:
            qs[r - 3] = x.astype(jnp.bfloat16)
        x = rms_rows(side[r].astype(jnp.float32), gain)
        normed[r, 0:3, :] = x[5:8]
        normed[r, 3 + breadth:6 + breadth, :] = x[0:3]
    q = jnp.dot(qs[...].reshape(ROWS * breadth, channels), wq_ref[...], preferred_element_type=jnp.float32)
    qs[...] = (q.astype(jnp.bfloat16) * jnp.bfloat16(0.125)).reshape(ROWS, breadth, channels)
    flat = normed[...].reshape(SPAN * wide, channels).astype(jnp.bfloat16)
    kv[:, :, :channels] = jnp.dot(flat, wk_ref[...], preferred_element_type=jnp.float32).reshape(SPAN, wide, channels)
    kv[:, :, channels:] = jnp.dot(flat, wv_ref[...], preferred_element_type=jnp.float32).reshape(SPAN, wide, channels)
    row0, col0, height, width = place_ref[0], place_ref[1], place_ref[2], place_ref[3]
    krow = keyrow_ref[...] + row0
    row_ok = (krow >= 0) & (krow < height)
    low = lax.broadcasted_iota(jnp.int32, (ROWS * QC, 128), 1) < 64
    ones = jnp.ones((SPAN * KC, 128), jnp.bfloat16)

    def block(cb, carry):
        c0 = pl.multiple_of(cb * QC, QC)
        kcol = keycol_ref[...] + (col0 + c0)
        ok = row_ok & (kcol >= 0) & (kcol < width)
        bias = inside_ref[...] + jnp.where(ok, 0.0, -jnp.inf)
        bias = jnp.concatenate([bias, bias], axis=0)
        for pair in range(channels // 128):
            lanes = slice(128 * pair, 128 * pair + 128)
            qp = qs[:, pl.ds(c0, QC), lanes].reshape(ROWS * QC, 128)
            zero = jnp.zeros_like(qp)
            q2 = jnp.concatenate([jnp.where(low, qp, zero), jnp.where(low, zero, qp)], axis=0)
            kp = kv[:, pl.ds(c0, KC), lanes].reshape(SPAN * KC, 128).astype(jnp.bfloat16)
            vp = kv[:, pl.ds(c0, KC), channels + 128 * pair:channels + 128 * pair + 128].reshape(SPAN * KC, 128).astype(jnp.bfloat16)
            s = lax.dot_general(q2, kp, (((1,), (1,)), ((), ())), preferred_element_type=jnp.float32) + bias
            p = jnp.exp(s - jnp.max(s, axis=-1, keepdims=True)).astype(jnp.bfloat16)
            o = jnp.dot(p, jnp.concatenate([vp, ones], axis=1), preferred_element_type=jnp.float32)
            half = ROWS * QC
            num = jnp.where(low, o[:half, :128], o[half:, :128])
            den = jnp.where(low, o[:half, 128:], o[half:, 128:])
            mix[:, pl.ds(c0, QC), lanes] = (num / den).astype(jnp.bfloat16).reshape(ROWS, QC, 128)
        return carry

    lax.fori_loop(0, breadth // QC, block, 0)
    out = jnp.dot(mix[...].reshape(ROWS * breadth, channels), wo_ref[...], preferred_element_type=jnp.float32)
    out_ref[...] = (tok[3:3 + ROWS].astype(jnp.float32).reshape(ROWS * breadth, channels) + out).astype(jnp.bfloat16)

def window_call(place, gain, wq, wk, wv, wo, parts):
    plan, srcs, edges, at = [], [], [], 0
    for array, edge, first, count in parts:
        plan.append((at, first, count))
        srcs.append(array)
        edges.append(edge)
        at += count
    breadth, channels = srcs[0].shape[1:]
    wide = breadth + 8
    n = np.arange(SPAN * KC)
    m = np.arange(ROWS * QC)
    rg = n[None] // KC - m[:, None] // QC
    cg = n[None] % KC - m[:, None] % QC
    inside = np.where((rg >= 0) & (rg <= 6) & (cg >= 0) & (cg <= 6), 0.0, -np.inf).astype(np.float32)
    keyrow = (n // KC - 3).astype(np.int32)[None]
    keycol = (n % KC - 3).astype(np.int32)[None]
    vm = pl.BlockSpec(memory_space=pltpu.VMEM)
    return pl.pallas_call(
        functools.partial(window_kernel, tuple(plan)),
        out_shape=jax.ShapeDtypeStruct((ROWS * breadth, channels), jnp.bfloat16),
        in_specs=[pl.BlockSpec(memory_space=pltpu.SMEM)] + [vm] * 8 + [pl.BlockSpec(memory_space=pl.ANY)] * (2 * len(srcs)),
        out_specs=vm,
        scratch_shapes=[
            pltpu.VMEM((SPAN, breadth, channels), jnp.bfloat16),
            pltpu.VMEM((SPAN, 8, channels), jnp.bfloat16),
            pltpu.VMEM((SPAN, wide, channels), jnp.float32),
            pltpu.VMEM((ROWS, breadth, channels), jnp.bfloat16),
            pltpu.VMEM((SPAN, wide, 2 * channels), jnp.float32),
            pltpu.VMEM((ROWS, breadth, channels), jnp.bfloat16),
            pltpu.SemaphoreType.DMA((2 * len(srcs),)),
        ],
        compiler_params=pltpu.CompilerParams(vmem_limit_bytes=48 << 20),
    )(place, jnp.asarray(inside), jnp.asarray(keyrow), jnp.asarray(keycol), gain.reshape(1, -1), wq, wk, wv, wo, *srcs, *edges)


TILE = 16

def gather_kernel(n_pieces, piece_rows, *refs):
    idx_ref, w_ref, qa_ref, ta_ref, sgain_ref, cgain_ref, wk_ref, wv_ref, wo_ref = refs[:9]
    pieces = refs[9:9 + n_pieces]
    joined_ref, normed_ref, stage, table, res, sems = refs[9 + n_pieces:]
    t = pl.program_id(0)
    tiles = pl.num_programs(0)
    breadth = tiles * TILE
    rows = TILE * TILE
    channels = res.shape[1]
    total = TILE * breadth

    @pl.when(t == 0)
    def _():
        slots = stage.shape[0]
        def copy(n):
            return pltpu.make_async_copy(pieces[n], stage.at[n % slots], sems.at[n % slots])
        for n in range(min(slots, n_pieces)):
            copy(n).start()
        for n in range(n_pieces):
            copy(n).wait()
            table[pl.ds(n * piece_rows, piece_rows), :] = stage[n % slots].astype(jnp.float32)
            if n + slots < n_pieces:
                copy(n + slots).start()

    def line(i, carry):
        base = i * breadth + t * TILE
        out0 = pl.multiple_of(i * TILE, TILE)
        for j in range(TILE):
            acc = None
            for k in range(4):
                at = k * total + base + j
                term = w_ref[at] * table[pl.ds(idx_ref[at], 1), :]
                acc = term if acc is None else acc + term
            res[pl.ds(out0 + j, 1), :] = acc
        return carry

    lax.fori_loop(0, TILE, line, 0)
    r = res[...].astype(jnp.bfloat16).astype(jnp.float32)
    nr = rms_rows(r, sgain_ref[...]).astype(jnp.bfloat16)
    kk = jnp.dot(nr, wk_ref[...], preferred_element_type=jnp.float32).astype(jnp.bfloat16)
    vv = jnp.dot(nr, wv_ref[...], preferred_element_type=jnp.float32).astype(jnp.bfloat16)
    qa = qa_ref[...].reshape(rows, channels)
    ones = jnp.ones((rows, 128), jnp.bfloat16)
    part = 128
    low = lax.broadcasted_iota(jnp.int32, (part, 128), 1) < 64
    mixes = []
    for pair in range(channels // 128):
        lanes = slice(128 * pair, 128 * pair + 128)
        kp, v2 = kk[:, lanes], jnp.concatenate([vv[:, lanes], ones], axis=1)
        halves = []
        for q0 in range(0, rows, part):
            qp = qa[q0:q0 + part, lanes]
            zero = jnp.zeros_like(qp)
            q2 = jnp.concatenate([jnp.where(low, qp, zero), jnp.where(low, zero, qp)], axis=0)
            s = lax.dot_general(q2, kp, (((1,), (1,)), ((), ())), preferred_element_type=jnp.float32)
            p = jnp.exp(s - jnp.max(s, axis=-1, keepdims=True)).astype(jnp.bfloat16)
            o = jnp.dot(p, v2, preferred_element_type=jnp.float32)
            num = jnp.where(low, o[:part, :128], o[part:, :128])
            den = jnp.where(low, o[:part, 128:], o[part:, 128:])
            halves.append((num / den).astype(jnp.bfloat16))
        mixes.append(jnp.concatenate(halves, axis=0))
    mix = jnp.concatenate(mixes, axis=1)
    out = jnp.dot(mix, wo_ref[...], preferred_element_type=jnp.float32)
    joined = (ta_ref[...].reshape(rows, channels).astype(jnp.float32) + out).astype(jnp.bfloat16)
    joined_ref[...] = joined.reshape(TILE, TILE, channels)
    normed_ref[...] = rms_rows(joined.astype(jnp.float32), cgain_ref[...]).astype(jnp.bfloat16).reshape(TILE, TILE, channels)

def gather_call(idx, weights, qa, ta, sgain, cgain, wk, wv, wo, pieces):
    height, breadth, channels = ta.shape
    piece_rows = pieces[0].shape[0]
    n = len(pieces)
    sm = pl.BlockSpec(memory_space=pltpu.SMEM)
    vm = pl.BlockSpec(memory_space=pltpu.VMEM)
    tile = pl.BlockSpec((TILE, TILE, channels), lambda t: (0, t, 0))
    shape = jax.ShapeDtypeStruct((height, breadth, channels), jnp.bfloat16)
    return pl.pallas_call(
        functools.partial(gather_kernel, n, piece_rows),
        grid=(breadth // TILE,),
        out_shape=(shape, shape),
        in_specs=[sm, sm, tile, tile] + [vm] * 5 + [pl.BlockSpec(memory_space=pl.ANY)] * n,
        out_specs=(tile, tile),
        scratch_shapes=[
            pltpu.VMEM((8, piece_rows, channels), jnp.bfloat16),
            pltpu.VMEM((n * piece_rows, channels), jnp.float32),
            pltpu.VMEM((TILE * TILE, channels), jnp.float32),
            pltpu.SemaphoreType.DMA((8,)),
        ],
        compiler_params=pltpu.CompilerParams(vmem_limit_bytes=48 << 20),
    )(idx, weights, qa, ta, sgain.reshape(1, -1), cgain.reshape(1, -1), wk, wv, wo, *pieces)


SIDE = 8

def gelu(x):
    return 0.5 * x * (1.0 + jnp.tanh(0.7978845608028654 * (x + 0.044715 * (x * x * x))))

def conv_rows(src, row, count, w_ref):
    span, channels = src.shape[1], src.shape[2]
    lhs = jnp.concatenate([src[row + a:row + a + count] if isinstance(row, int) else src[pl.ds(row + a, count)] for a in range(3)], axis=-1)
    y = jnp.dot(lhs.reshape(count * span, 3 * channels), w_ref[...], preferred_element_type=jnp.float32)
    y = y.reshape(count * span, 3 * channels)
    n = count * span
    return (pltpu.roll(y[:, :channels], 1, 0) + y[:, channels:2 * channels]
            + pltpu.roll(y[:, 2 * channels:], n - 1, 0)).reshape(count, span, channels)

def conv_kernel(place_ref, nc_ref, top_ref, bot_ref, side_ref, side_top_ref, side_bot_ref, joined_ref, w1_hbm, w2_hbm, out_ref,
                field, inner, w1, w2, sems):
    height, breadth, channels = nc_ref.shape
    span = field.shape[1]
    copies = []
    for n, (src, dst) in enumerate(((w1_hbm, w1), (w2_hbm, w2))):
        for a in range(3):
            for b in range(3):
                copies.append(pltpu.make_async_copy(
                    src.at[a, b], dst.at[pl.ds(a * channels, channels), pl.ds(b * channels, channels)],
                    sems.at[9 * n + 3 * a + b]))
    for c in copies:
        c.start()
    field[2:2 + height, SIDE:SIDE + breadth, :] = nc_ref[...]
    field[0:2, SIDE:SIDE + breadth, :] = top_ref[...]
    field[2 + height:4 + height, SIDE:SIDE + breadth, :] = bot_ref[...]
    row0, col0, total_h, total_w = place_ref[0], place_ref[1], place_ref[2], place_ref[3]
    for first_row, ref in ((0, side_top_ref), (2, side_ref), (2 + height, side_bot_ref)):
        edge = ref[...]
        zero = jnp.zeros_like(edge)
        rows = slice(first_row, first_row + edge.shape[0])
        field[rows, 0:SIDE, :] = jnp.where(col0 > 0, edge, zero)
        field[rows, SIDE + breadth:, :] = jnp.where(col0 + breadth < total_w, edge, zero)
    for c in copies[:9]:
        c.wait()
    col = lax.broadcasted_iota(jnp.int32, (1, span, 1), 1) + (col0 - SIDE)
    col_ok = (col >= 0) & (col < total_w)
    step1 = 3

    def first(n, carry):
        r = n * step1
        x = gelu(conv_rows(field, r, step1, w1))
        row = lax.broadcasted_iota(jnp.int32, (step1, 1, 1), 0) + (row0 - 1 + r)
        ok = (row >= 0) & (row < total_h) & col_ok
        inner[pl.ds(r, step1)] = jnp.where(ok, x, 0.0).astype(jnp.bfloat16)
        return carry

    lax.fori_loop(0, (height + 2) // step1, first, 0)
    for c in copies[9:]:
        c.wait()
    step2 = 4

    def second(n, carry):
        r = n * step2
        y = conv_rows(inner, r, step2, w2)[:, SIDE:SIDE + breadth, :]
        out_ref[pl.ds(r, step2)] = (joined_ref[pl.ds(r, step2)].astype(jnp.float32) + y).astype(jnp.bfloat16)
        return carry

    lax.fori_loop(0, height // step2, second, 0)

def conv_call(place, nc, top, bot, side, side_top, side_bot, joined, w1, w2):
    height, breadth, channels = nc.shape
    span = breadth + 2 * SIDE
    sm = pl.BlockSpec(memory_space=pltpu.SMEM)
    vm = pl.BlockSpec(memory_space=pltpu.VMEM)
    hb = pl.BlockSpec(memory_space=pl.ANY)
    return pl.pallas_call(
        conv_kernel,
        out_shape=jax.ShapeDtypeStruct(nc.shape, jnp.bfloat16),
        in_specs=[sm] + [vm] * 7 + [hb] * 2,
        out_specs=vm,
        scratch_shapes=[
            pltpu.VMEM((height + 4, span, channels), jnp.bfloat16),
            pltpu.VMEM((height + 2, span, channels), jnp.bfloat16),
            pltpu.VMEM((3 * channels, 3 * channels), jnp.bfloat16),
            pltpu.VMEM((3 * channels, 3 * channels), jnp.bfloat16),
            pltpu.SemaphoreType.DMA((18,)),
        ],
        compiler_params=pltpu.CompilerParams(vmem_limit_bytes=48 << 20),
    )(place, nc, top, bot, side, side_top, side_bot, joined, w1, w2)

def index_kernel(place_ref, slots_ref, weights_ref, tables_ref, index_ref, live_ref):
    swath, group, groups, cap, block = (place_ref[n] for n in range(5))
    lines = tables_ref.shape[1] - 1
    slots = slots_ref[...]
    peer, place = lax.div(slots, cap), lax.rem(slots, cap)
    step = lax.div(peer, groups) - swath
    other = jnp.where(lax.rem(peer, groups) == group, 0, 1)
    source = (step + 1) * 2 + other
    line, lane = source * lines + lax.div(place, 128), lax.rem(place, 128)
    cell = jnp.zeros_like(slots)
    count = jnp.zeros_like(slots)
    for s in range(6):
        count = jnp.where(source == s, jnp.broadcast_to(tables_ref[s, lines:lines + 1, :], slots.shape), count)
        for n in range(lines):
            row = jnp.broadcast_to(tables_ref[s, n:n + 1, :], slots.shape)
            picked = jnp.take_along_axis(row, lane, axis=1)
            cell = jnp.where(line == s * lines + n, picked, cell)
    toward = jnp.where(lax.rem(swath, 2) == 0, 1, -1)
    slot = jnp.where(step == 0, 0, jnp.where(step == toward, 1, 2))
    index_ref[...] = (slot * 2 + other) * block + cell
    live_ref[...] = jnp.where(place < count, weights_ref[...], 0.0)


def index_call(place, slots, weights, tables):
    sm = pl.BlockSpec(memory_space=pltpu.SMEM)
    vm = pl.BlockSpec(memory_space=pltpu.VMEM)
    return pl.pallas_call(
        index_kernel,
        out_shape=(jax.ShapeDtypeStruct(slots.shape, jnp.int32), jax.ShapeDtypeStruct(slots.shape, jnp.float32)),
        in_specs=[sm] + [vm] * 3,
        out_specs=(vm, vm),
    )(place, slots, weights, tables)


def rms_gain(values, gain_vector):
    return rms_rows(values.astype(jnp.float32), gain_vector).astype(jnp.bfloat16)


def body(
    tokens_b,
    tokens_a,
    pack_rows,
    pack_count,
    gather_slots,
    blend_weights,
    swath_gain,
    swath_query,
    swath_key,
    swath_value,
    swath_out,
    query_gain,
    source_gain,
    cross_query,
    cross_key,
    cross_value,
    cross_out,
    conv_gain,
    conv_first,
    conv_second,
):
    height, breadth, channels = tokens_b.shape
    swaths, groups = lax.axis_size("swath"), lax.axis_size("group")
    swath, group = lax.axis_index("swath"), lax.axis_index("group")
    assert groups == 2 and swaths % 2 == 0
    whole = [height * swaths, breadth * groups]
    down = [(i, i + 1) for i in range(swaths - 1)]
    up = [(j, i) for i, j in down]
    swap = [(0, 1), (1, 0)]
    pairs = [(i, i ^ 1) for i in range(swaths)]
    relay = [(i, j) for i in range(swaths) for j in [i + 2 if i % 2 == 0 else i - 2] if 0 <= j < swaths]
    cross = lambda moves: [(2 * i + g, 2 * j + 1 - g) for i, j in moves for g in (0, 1)]

    def inner_edge(field):
        start = (1 - group) * (breadth - SIDE)
        return lax.dynamic_slice_in_dim(field, start, SIDE, axis=1)

    def rims(field, width):
        edge = inner_edge(field)
        last, first = slice(height - width, height), slice(0, width)
        return (
            lax.ppermute(edge, "group", swap),
            lax.ppermute(field[last], "swath", down),
            lax.ppermute(field[first], "swath", up),
            lax.ppermute(edge[last], ("swath", "group"), cross(down)),
            lax.ppermute(edge[first], ("swath", "group"), cross(up)),
        )

    side, top, bottom, side_top, side_bottom = rims(tokens_b, 3)
    parts = {
        0: [(top, side_top, 0, 3), (tokens_b, side, 0, SPAN - 3)],
        height - ROWS: [(tokens_b, side, height - ROWS - 3, ROWS + 3), (bottom, side_bottom, 0, 3)],
    }
    chunks = {}
    order = [r for r in range(ROWS, height - ROWS, ROWS)] + [0, height - ROWS]
    for r in order:
        place = jnp.stack([swath * height + r, group * breadth, jnp.int32(whole[0]), jnp.int32(whole[1])]).astype(jnp.int32)
        chunks[r] = window_call(
            place, swath_gain, swath_query, swath_key, swath_value, swath_out,
            parts.get(r, [(tokens_b, side, r - 3, SPAN)]),
        )
    blocks = [{}, {}, {}]
    for r in order:
        mine = chunks[r]
        near = lax.ppermute(mine, "swath", pairs)
        far = lax.ppermute(near, "swath", relay)
        for at, rows in enumerate((mine, near, far)):
            blocks[at][r] = (rows, lax.ppermute(rows, "group", swap))
    pieces = [blocks[at][r][o] for at in range(3) for o in range(2) for r in sorted(order)]

    cap = pack_rows.shape[-1]
    lines = cap // 128
    tables = jnp.concatenate(
        [pack_rows.reshape(-1, lines, 128), jnp.broadcast_to(pack_count.reshape(-1, 1, 1), (pack_count.size, 1, 128))], axis=1
    ).reshape(swaths, groups, lines + 1, 128)
    pick = lambda step: lax.dynamic_index_in_dim(tables, jnp.clip(swath + step, 0, swaths - 1), 0, keepdims=False)
    held = jnp.stack([lax.ppermute(pick(1), "swath", down), pick(0), lax.ppermute(pick(-1), "swath", up)])
    here = lax.dynamic_index_in_dim(held, group, 1, keepdims=False)
    there = lax.ppermute(lax.dynamic_index_in_dim(held, 1 - group, 1, keepdims=False), "group", swap)
    tables = jnp.stack([here, there], axis=1).reshape(6, lines + 1, 128)
    place = jnp.stack([swath, group, jnp.int32(groups), jnp.int32(cap), jnp.int32(height * breadth)]).astype(jnp.int32)
    index, live = index_call(place, gather_slots.reshape(-1, 128), blend_weights.reshape(-1, 128), tables)

    normed_a = rms_gain(tokens_a, query_gain).reshape(-1, channels)
    query_a = jnp.dot(normed_a, cross_query, preferred_element_type=jnp.float32).astype(jnp.bfloat16)
    query_a = (query_a * jnp.bfloat16(0.125)).reshape(tokens_a.shape)
    joined, normed_c = gather_call(
        index.reshape(-1), live.reshape(-1), query_a, tokens_a, source_gain, conv_gain,
        cross_key, cross_value, cross_out, pieces,
    )
    side, top, bottom, side_top, side_bottom = rims(normed_c, 2)
    place = jnp.stack([swath * height, group * breadth, jnp.int32(whole[0]), jnp.int32(whole[1])]).astype(jnp.int32)
    return conv_call(place, normed_c, top, bottom, side, side_top, side_bottom, joined, conv_first, conv_second)


def solution(mesh):
    rows = P(("strip", "swath"), "group", None)
    maps = P(None, ("strip", "swath"), "group")
    placed = (rows, rows, P(("strip", "swath"), "group", None, None), rows, maps, maps) + (P(),) * 14
    return jax.shard_map(body, mesh=mesh, in_specs=placed, out_specs=rows, check_vma=False)
```

time: 705 us -> 215 us (0.30)
  local copies, waits for them, and re-layouts: 421 us -> 23.2 us
  Pallas kernels: 0 us -> 105 us
  matrix products: 98.8 us -> 2.29 us
  other arithmetic: 62 us -> 4.5 us
  waiting for transfers between devices: 65.2 us -> 16.7 us
  starting transfers between devices: 39 us -> 58.9 us
  blocking collectives: 7.51 us -> 0 us
    gather x295 -> x0, local copies, waits for them, and re-layouts: 336 us -> none
    pallas_call x0 -> x7, Pallas kernels: none -> 105 us  [the longest x4 40.2 us: window_call(): pl.pallas_call(functools.partial(window_kernel, tuple(plan)), out_shape=j...]
    dot_general x30 -> x1, matrix products: 98.8 us -> 2.29 us  [body(): jnp.dot(normed_a, cross_query, preferred_element_type=jnp.float32)]
    ppermute x14 -> x33, waiting for transfers between devices: 65.2 us -> 16.7 us  [the longest x4 14.2 us: body(): far = lax.ppermute(near, 'swath', relay)]
    reshape x6 -> x3, local copies, waits for them, and re-layouts: 34.1 us -> 0.01 us  [the longest x1 0.01 us: gather_call(): sgain.reshape(1, -1)]
    sub x2 -> x0, other arithmetic: 31.8 us -> none  [the longest x1 15.9 us: attend_group(): raised = jnp.exp(scores - row_peak)]
    another operation x5 -> x1, local copies, waits for them, and re-layouts: 22.2 us -> 0.63 us  [body(): jnp.stack([swath, group, jnp.int32(groups), jnp.int32(cap), jnp.int32(hei...]
    ppermute x14 -> x33, starting transfers between devices: 39 us -> 58.9 us  [the longest x4 11.2 us: body(): far = lax.ppermute(near, 'swath', relay)]
  transfers between devices with their start and end apart: 14 -> 33, of which waited for: 5 -> 6; matrix products, arithmetic and copies ran while one was open for 13% -> 6% of each run, Pallas kernels for 0% -> 20%
where the time goes in v1:
time: 215 us; the launch traced here: 211 us
  Pallas kernels  105 us (49%)
  starting transfers between devices  58.9 us (27%)
  local copies, waits for them, and re-layouts  23.2 us (11%)
  waiting for transfers between devices  16.7 us (8%)
  other arithmetic  4.5 us (2%)
  matrix products  2.29 us (1%)
    pallas_call x4, Pallas kernels, window_call(): pl.pallas_call(functools.partial(window_kernel, tuple(plan)), out_shape=j...  40.2 us
    pallas_call x1, Pallas kernels, gather_call(): pl.pallas_call(functools.partial(gather_kernel, n, piece_rows), grid=(bre...  39.2 us
    pallas_call x1, Pallas kernels, conv_call(): pl.pallas_call(conv_kernel, out_shape=jax.ShapeDtypeStruct(nc.shape, jnp....  22.7 us
    unnamed x76, local copies, waits for them, and re-layouts  14.9 us
    ppermute x4, waiting for transfers between devices, body(): far = lax.ppermute(near, 'swath', relay)  14.2 us
    ppermute x4, starting transfers between devices, body(): far = lax.ppermute(near, 'swath', relay)  11.2 us
    ppermute x12, starting transfers between devices, body(): blocks[at][r] = (rows, lax.ppermute(rows, 'group', swap))  10.7 us
    ppermute x2, starting transfers between devices, rims(): lax.ppermute(field[first], 'swath', up)  8 us
  transfers between devices with their start and end apart: 33, of which 6 were waited for; matrix products, arithmetic and copies ran while one was open for 6% of the time, Pallas kernels for 20%

profile of v1, /device:TPU:11, one launch (start us, length us, event | category | flops | bytes accessed | tf_op | source)
XLA Modules:
  0.0 211.5 jit_solution(1072957435562456138)
XLA Ops:
  0.1 1.0 copy.33
  1.6 1.3 reduce.3
  3.1 3.1 %collective-permute-start = (s32[2,9,128]{2,1,0:T(8,128)S(1)}, s32[2,9,128]{2,1,0:T(8,128)S(1)}, u32[]{:S(2)}, u32[]{:S(2)}) collective-permute-start(s32[2,9,128]{2,1,0:T(8,128)S(1)} %get-tuple-element.21), channel_id=1, source_target_pairs={{0,2},{2,4},{4,6},{6,8},{8,10},{10,12},{12,14},{1,3},{3,5},{5,7},{... | collective-permute-start | bytes 27656 | tf_op jit(solution)/shard_map/ppermute | solution.py:413
  6.2 3.0 %collective-permute-start.1 = (s32[2,9,128]{2,1,0:T(8,128)S(1)}, s32[2,9,128]{2,1,0:T(8,128)S(1)}, u32[]{:S(2)}, u32[]{:S(2)}) collective-permute-start(s32[2,9,128]{2,1,0:T(8,128)S(1)} %get-tuple-element.23), channel_id=1, source_target_pairs={{2,0},{4,2},{6,4},{8,6},{10,8},{12,10},{14,12},{3,1},{5,3},{7,5},{... | collective-permute-start | bytes 27656 | tf_op jit(solution)/shard_map/ppermute | solution.py:413
  9.3 0.9 constant_dynamic-slice_fusion.5
  10.2 1.3 collective-permute-start.5
  11.5 1.4 constant_dynamic-slice_fusion.1
  12.9 2.1 %collective-permute-start.4 = (bf16[3,8,384]{2,1,0:T(8,128)(2,1)}, bf16[3,8,384]{2,1,0:T(8,128)(2,1)}, u32[]{:S(2)}, u32[]{:S(2)}) collective-permute-start(bf16[3,8,384]{2,1,0:T(8,128)(2,1)} %get-tuple-element.18), channel_id=1, source_target_pairs={{0,3},{1,2},{2,5},{3,4},{4,7},{5,6},{6,9},{7,8},{8,11},{9,10},{10,... | collective-permute-start | bytes 55304 | tf_op jit(solution)/shard_map/ppermute | solution.py:381
  15.0 1.9 fusion.10
  16.9 4.0 %collective-permute-start.3 = (bf16[3,128,384]{2,1,0:T(8,128)(2,1)}, bf16[3,128,384]{2,1,0:T(8,128)(2,1)}, u32[]{:S(2)}, u32[]{:S(2)}) collective-permute-start(bf16[3,128,384]{2,1,0:T(8,128)(2,1)} %get-tuple-element.20), channel_id=1, source_target_pairs={{0,2},{2,4},{4,6},{6,8},{8,10},{10,12},{12,14},{1,3},{3,5},{5,7},{... | collective-permute-start | bytes 884744 | tf_op jit(solution)/shard_map/ppermute | solution.py:379
  21.2 2.8 %collective-permute-start.7 = (bf16[3,8,384]{2,1,0:T(8,128)(2,1)}, bf16[3,8,384]{2,1,0:T(8,128)(2,1)S(1)}, u32[]{:S(2)}, u32[]{:S(2)}) collective-permute-start(bf16[3,8,384]{2,1,0:T(8,128)(2,1)} %get-tuple-element.17), channel_id=1, source_target_pairs={{2,1},{3,0},{4,3},{5,2},{6,5},{7,4},{8,7},{9,6},{10,9},{11,8},{12,... | collective-permute-start | bytes 55304 | tf_op jit(solution)/shard_map/ppermute | solution.py:382
  24.0 3.7 %collective-permute-start.6 = (bf16[3,128,384]{2,1,0:T(8,128)(2,1)}, bf16[3,128,384]{2,1,0:T(8,128)(2,1)S(1)}, u32[]{:S(2)}, u32[]{:S(2)}) collective-permute-start(bf16[3,128,384]{2,1,0:T(8,128)(2,1)} %get-tuple-element.19), channel_id=1, source_target_pairs={{2,0},{4,2},{6,4},{8,6},{10,8},{12,10},{14,12},{3,1},{5,3},{7,5},{... | collective-permute-start | bytes 884744 | tf_op jit(solution)/shard_map/ppermute | solution.py:380
  27.7 0.6 constant_dynamic-slice_fusion.6
  28.5 1.0 copy-done.3
  29.5 1.0 copy-done.5
  30.4 1.0 copy-done.7
  31.4 9.5 %shard_map.300.refs_10_ = bf16[512,384]{1,0:T(8,128)(2,1)S(1)} custom-call(s32[4]{0:T(128)S(1)} %pad_add_fusion.4.place_ref, f32[64,240]{1,0:T(8,128)S(1)} %copy-done.13, s32[1,240]{1,0:T(1,128)S(1)} %copy-done.25, s32[1,240]{1,0:T(1,128)S(1)} %copy-done.26, f32[1,384]{1,0:T(1,128)S(1)} %reshape.62.gain_ref, bf16[384,384]{1,0:T(8,128)(2,1)S(1)} %copy-done.2, ...), custom_call_target="tpu_custom_call" | custom-call | tf_op jit(solution)/shard_map/pallas_call | solution.py:102
  40.9 10.3 %shard_map.301.refs_11_ = bf16[512,384]{1,0:T(8,128)(2,1)} custom-call(s32[4]{0:T(128)S(1)} %pad_add_fusion.3.place_ref, f32[64,240]{1,0:T(8,128)S(1)} %copy-done.13, s32[1,240]{1,0:T(1,128)S(1)} %copy-done.25, s32[1,240]{1,0:T(1,128)S(1)} %copy-done.26, f32[1,384]{1,0:T(1,128)S(1)} %reshape.62.gain_ref, bf16[384,384]{1,0:T(8,128)(2,1)S(1)} %copy-done.2, ...), custom_call_target="tpu_custom_call" | custom-call | tf_op jit(solution)/shard_map/pallas_call | solution.py:102
  51.3 1.4 collective-permute-start.14
  52.8 10.9 %shard_map.299.refs_9_ = bf16[512,384]{1,0:T(8,128)(2,1)} custom-call(s32[4]{0:T(128)S(1)} %pad_add_fusion.5.place_ref, f32[64,240]{1,0:T(8,128)S(1)} %copy-done.14, s32[1,240]{1,0:T(1,128)S(1)} %copy-done.25, s32[1,240]{1,0:T(1,128)S(1)} %copy-done.26, f32[1,384]{1,0:T(1,128)S(1)} %reshape.62.gain_ref, bf16[384,384]{1,0:T(8,128)(2,1)S(1)} %copy-done.2, ...), custom_call_target="tpu_custom_call" | custom-call | tf_op jit(solution)/shard_map/pallas_call | solution.py:102
  63.7 0.6 copy-done.23
  64.2 1.0 collective-permute-start.10
  65.9 0.7 copy-done.19
  66.7 0.8 copy-done.15
  67.5 1.0 copy-done.20
  68.5 0.7 copy-done.24
  69.2 9.5 %shard_map.302.refs_12_ = bf16[512,384]{1,0:T(8,128)(2,1)S(1)} custom-call(s32[4]{0:T(128)S(1)} %pad_add_fusion.2.place_ref, f32[64,240]{1,0:T(8,128)S(1)} %copy-done.15, s32[1,240]{1,0:T(1,128)S(1)} %copy-done.25, s32[1,240]{1,0:T(1,128)S(1)} %copy-done.26, f32[1,384]{1,0:T(1,128)S(1)} %reshape.62.gain_ref, bf16[384,384]{1,0:T(8,128)(2,1)S(1)} %copy-done.2, ...), custom_call_target="tpu_custom_call" | custom-call | tf_op jit(solution)/shard_map/pallas_call | solution.py:102
  78.8 1.5 collective-permute-start.15
  81.0 0.8 copy-done.10
  81.8 2.5 %collective-permute-start.21 = (bf16[512,384]{1,0:T(8,128)(2,1)}, bf16[512,384]{1,0:T(8,128)(2,1)}, u32[]{:S(2)}, u32[]{:S(2)}) collective-permute-start(bf16[512,384]{1,0:T(8,128)(2,1)} %collective-permute-done.13.refs_18_), channel_id=1, source_target_pairs={{0,4},{4,8},{6,2},{8,12},{10,6},{14,10},{1,5},{5,9},{7,3},{9,13},{... | collective-permute-start | bytes 1179656 | tf_op jit(solution)/shard_map/ppermute | solution.py:402
  84.3 3.4 %collective-permute-start.22 = (bf16[512,384]{1,0:T(8,128)(2,1)}, bf16[512,384]{1,0:T(8,128)(2,1)}, u32[]{:S(2)}, u32[]{:S(2)}) collective-permute-start(bf16[512,384]{1,0:T(8,128)(2,1)} %collective-permute-done.14.refs_19_), channel_id=1, source_target_pairs={{0,4},{4,8},{6,2},{8,12},{10,6},{14,10},{1,5},{5,9},{7,3},{9,13},{... | collective-permute-start | bytes 1179656 | tf_op jit(solution)/shard_map/ppermute | solution.py:402
  88.1 1.6 collective-permute-done.15.refs_20_
  89.7 0.8 collective-permute-start.17
  90.4 2.8 %collective-permute-start.20 = (bf16[512,384]{1,0:T(8,128)(2,1)}, bf16[512,384]{1,0:T(8,128)(2,1)}, u32[]{:S(2)}, u32[]{:S(2)}) collective-permute-start(bf16[512,384]{1,0:T(8,128)(2,1)} %collective-permute-done.12.refs_17_), channel_id=1, source_target_pairs={{0,4},{4,8},{6,2},{8,12},{10,6},{14,10},{1,5},{5,9},{7,3},{9,13},{... | collective-permute-start | bytes 1179656 | tf_op jit(solution)/shard_map/ppermute | solution.py:402
  93.3 0.9 collective-permute-done.21.refs_26_
  94.2 2.2 %collective-permute-start.16 = (bf16[512,384]{1,0:T(8,128)(2,1)}, bf16[512,384]{1,0:T(8,128)(2,1)S(1)}, u32[]{:S(2)}, u32[]{:S(2)}) collective-permute-start(bf16[512,384]{1,0:T(8,128)(2,1)} %collective-permute-done.12.refs_17_), channel_id=1, source_target_pairs={{0,1},{1,0},{2,3},{3,2},{4,5},{5,4},{6,7},{7,6},{8,9},{9,8},{10,11... | collective-permute-start | bytes 1179656 | tf_op jit(solution)/shard_map/ppermute | solution.py:404
  96.4 6.3 %collective-permute-done.22.refs_27_ = bf16[512,384]{1,0:T(8,128)(2,1)} collective-permute-done((bf16[512,384]{1,0:T(8,128)(2,1)}, bf16[512,384]{1,0:T(8,128)(2,1)}, u32[]{:S(2)}, u32[]{:S(2)}) %collective-permute-start.22) | collective-permute-done | bytes 393248 | tf_op jit(solution)/shard_map/ppermute | solution.py:402
  102.6 2.5 %collective-permute-start.23 = (bf16[512,384]{1,0:T(8,128)(2,1)S(1)}, bf16[512,384]{1,0:T(8,128)(2,1)}, u32[]{:S(2)}, u32[]{:S(2)}) collective-permute-start(bf16[512,384]{1,0:T(8,128)(2,1)S(1)} %collective-permute-done.15.refs_20_), channel_id=1, source_target_pairs={{0,4},{4,8},{6,2},{8,12},{10,6},{14,10},{1,5},{5,9},{7,3},{9,13},{... | collective-permute-start | bytes 1179656 | tf_op jit(solution)/shard_map/ppermute | solution.py:402
  105.2 0.6 stack.64.place_ref
  105.8 1.8 fusion.2
  107.7 2.5 %collective-permute-start.19 = (bf16[512,384]{1,0:T(8,128)(2,1)S(1)}, bf16[512,384]{1,0:T(8,128)(2,1)}, u32[]{:S(2)}, u32[]{:S(2)}) collective-permute-start(bf16[512,384]{1,0:T(8,128)(2,1)S(1)} %collective-permute-done.15.refs_20_), channel_id=1, source_target_pairs={{0,1},{1,0},{2,3},{3,2},{4,5},{5,4},{6,7},{7,6},{8,9},{9,8},{10,11... | collective-permute-start | bytes 1179656 | tf_op jit(solution)/shard_map/ppermute | solution.py:404
  110.3 0.7 collective-permute-done.20.refs_25_
  111.0 2.2 %collective-permute-start.26 = (bf16[512,384]{1,0:T(8,128)(2,1)}, bf16[512,384]{1,0:T(8,128)(2,1)}, u32[]{:S(2)}, u32[]{:S(2)}) collective-permute-start(bf16[512,384]{1,0:T(8,128)(2,1)} %collective-permute-done.22.refs_27_), channel_id=1, source_target_pairs={{0,1},{1,0},{2,3},{3,2},{4,5},{5,4},{6,7},{7,6},{8,9},{9,8},{10,11... | collective-permute-start | bytes 1179656 | tf_op jit(solution)/shard_map/ppermute | solution.py:404
  113.2 6.3 %collective-permute-done.23.refs_28_ = bf16[512,384]{1,0:T(8,128)(2,1)} collective-permute-done((bf16[512,384]{1,0:T(8,128)(2,1)S(1)}, bf16[512,384]{1,0:T(8,128)(2,1)}, u32[]{:S(2)}, u32[]{:S(2)}) %collective-permute-start.23) | collective-permute-done | bytes 393248 | tf_op jit(solution)/shard_map/ppermute | solution.py:402
  119.5 1.3 collective-permute-start.24
  120.8 2.3 %fusion.3 = bf16[2048,384]{1,0:T(8,128)(2,1)} fusion(bf16[2048,384]{1,0:T(8,128)(2,1)S(1)} %bitcast.33, bf16[384,384]{1,0:T(8,128)(2,1)S(1)} %copy-done), kind=kOutput, calls=%fused_computation.6 | convolution fusion | flops 605552640 | bytes 3440640 | tf_op jit(solution)/shard_map/dot_general | solution.py:421
  123.1 0.6 pad_add_fusion.1
  123.8 2.9 %shard_map.298 = (s32[64,128]{1,0:T(8,128)}, f32[64,128]{1,0:T(8,128)}) custom-call(s32[5]{0:T(128)} %stack.64.place_ref, s32[64,128]{1,0:T(8,128)} %bitcast.37, f32[64,128]{1,0:T(8,128)} %bitcast.38, s32[6,9,128]{2,1,0:T(8,128)} %bitcast.35), custom_call_target="tpu_custom_call" | custom-call | tf_op jit(solution)/shard_map/pallas_call | solution.py:324
  126.8 1.0 copy-done.18
  127.7 0.8 copy-done.21
  128.5 0.8 copy-done.22
  129.2 39.2 %shard_map.303 = (bf16[16,128,384]{2,1,0:T(8,128)(2,1)}, bf16[16,128,384]{2,1,0:T(8,128)(2,1)}) custom-call(s32[8192]{0:T(1024)S(1)} %bitcast.30, f32[8192]{0:T(1024)S(1)} %bitcast.31, bf16[16,128,384]{2,1,0:T(8,128)(2,1)} %bitcast.32, bf16[16,128,384]{2,1,0:T(8,128)(2,1)} %refs_3_.1, f32[1,384]{1,0:T(1,128)S(1)} %reshape.60.refs_4_, ...), custom_call_target="tpu_custom_call" | custom-call | tf_op jit(solution)/shard_map/pallas_call | solution.py:197
  168.4 1.1 fusion.9
  169.5 1.9 collective-permute-start.28
  171.4 4.3 %collective-permute-start.29 = (bf16[2,128,384]{2,1,0:T(8,128)(2,1)S(1)}, bf16[2,128,384]{2,1,0:T(8,128)(2,1)S(1)}, u32[]{:S(2)}, u32[]{:S(2)}) collective-permute-start(bf16[2,128,384]{2,1,0:T(8,128)(2,1)S(1)} %get-tuple-element.15), channel_id=1, source_target_pairs={{2,0},{4,2},{6,4},{8,6},{10,8},{12,10},{14,12},{3,1},{5,3},{7,5},{... | collective-permute-start | bytes 589832 | tf_op jit(solution)/shard_map/ppermute | solution.py:380
  175.7 0.9 constant_dynamic-slice_fusion.4
  176.6 1.1 collective-permute-start.30
  177.7 0.7 constant_dynamic-slice_fusion.2
  178.4 1.9 collective-permute-start.31
  180.4 4.5 %collective-permute-start.32 = (bf16[2,8,384]{2,1,0:T(8,128)(2,1)S(1)}, bf16[2,8,384]{2,1,0:T(8,128)(2,1)S(1)}, u32[]{:S(2)}, u32[]{:S(2)}) collective-permute-start(bf16[2,8,384]{2,1,0:T(8,128)(2,1)S(1)} %get-tuple-element.13), channel_id=1, source_target_pairs={{2,1},{3,0},{4,3},{5,2},{6,5},{7,4},{8,7},{9,6},{10,9},{11,8},{12,... | collective-permute-start | bytes 36872 | tf_op jit(solution)/shard_map/ppermute | solution.py:382
  184.9 0.8 collective-permute-done.32.side_bot_ref
  185.7 1.4 copy-done.9
  187.1 1.4 copy-done.12
  188.5 22.7 %shard_map.304 = bf16[16,128,384]{2,1,0:T(8,128)(2,1)} custom-call(s32[4]{0:T(128)S(1)} %pad_add_fusion.5.place_ref, bf16[16,128,384]{2,1,0:T(8,128)(2,1)S(1)} %copy-done.9, bf16[2,128,384]{2,1,0:T(8,128)(2,1)S(1)} %collective-permute-done.28.top_ref, bf16[2,128,384]{2,1,0:T(8,128)(2,1)S(1)} %collective-permute-done.29.bot_ref, ...), custom_call_target="tpu_custom_call" | custom-call | tf_op jit(solution)/shard_map/pallas_call | solution.py:283
  (110 shorter events, 3.0 us)
Async XLA Ops:
  0.0 120.8 %copy-start = (bf16[384,384]{1,0:T(8,128)(2,1)S(1)}, bf16[384,384]{1,0:T(8,128)(2,1)}, u32[]{:S(2)}) copy-start(bf16[384,384]{1,0:T(8,128)(2,1)} %param.45) | copy-start | bytes 884740
  0.0 28.4 %copy-start.13 = (f32[64,240]{1,0:T(8,128)S(1)}, f32[64,240]{1,0:T(8,128)}, u32[]{:S(2)}) copy-start(f32[64,240]{1,0:T(8,128)} %constant.73.clone.inside_ref) | copy-start | bytes 184324
  0.0 28.5 %copy-start.25 = (s32[1,240]{1,0:T(1,128)S(1)}, s32[1,240]{1,0:T(1,128)}, u32[]{:S(2)}) copy-start(s32[1,240]{1,0:T(1,128)} %constant.74.clone.keyrow_ref) | copy-start | bytes 2884
  0.0 28.5 %copy-start.26 = (s32[1,240]{1,0:T(1,128)S(1)}, s32[1,240]{1,0:T(1,128)}, u32[]{:S(2)}) copy-start(s32[1,240]{1,0:T(1,128)} %constant.75.clone.keycol_ref) | copy-start | bytes 2884
  0.0 28.5 %copy-start.1 = (bf16[16,128,384]{2,1,0:T(8,128)(2,1)S(1)}, bf16[16,128,384]{2,1,0:T(8,128)(2,1)}, u32[]{:S(2)}) copy-start(bf16[16,128,384]{2,1,0:T(8,128)(2,1)} %rest_0_.5) | copy-start | bytes 4718596
  0.0 28.4 %copy-start.33 = (f32[384]{0:T(512)S(1)}, f32[384]{0:T(512)}, u32[]{:S(2)}) copy-start(f32[384]{0:T(512)} %param.38) | copy-start | bytes 4612
  0.0 28.4 %copy-start.2 = (bf16[384,384]{1,0:T(8,128)(2,1)S(1)}, bf16[384,384]{1,0:T(8,128)(2,1)}, u32[]{:S(2)}) copy-start(bf16[384,384]{1,0:T(8,128)(2,1)} %wq_ref.7) | copy-start | bytes 884740
  3.1 18.1 %collective-permute-start = (s32[2,9,128]{2,1,0:T(8,128)S(1)}, s32[2,9,128]{2,1,0:T(8,128)S(1)}, u32[]{:S(2)}, u32[]{:S(2)}) collective-permute-start(s32[2,9,128]{2,1,0:T(8,128)S(1)} %get-tuple-element.21), channel_id=1, source_target_pairs={{0,2},{2,4},{4,6},{6,8},{8,10},{10,12},{12,14},{1,3},{3,5},{5,7},{... | collective-permute-start | bytes 27656 | tf_op jit(solution)/shard_map/ppermute | solution.py:413
  6.2 17.7 %collective-permute-start.1 = (s32[2,9,128]{2,1,0:T(8,128)S(1)}, s32[2,9,128]{2,1,0:T(8,128)S(1)}, u32[]{:S(2)}, u32[]{:S(2)}) collective-permute-start(s32[2,9,128]{2,1,0:T(8,128)S(1)} %get-tuple-element.23), channel_id=1, source_target_pairs={{2,0},{4,2},{6,4},{8,6},{10,8},{12,10},{14,12},{3,1},{5,3},{7,5},{... | collective-permute-start | bytes 27656 | tf_op jit(solution)/shard_map/ppermute | solution.py:413
  10.2 18.1 %collective-permute-start.5 = (bf16[16,8,384]{2,1,0:T(8,128)(2,1)S(1)}, bf16[16,8,384]{2,1,0:T(8,128)(2,1)S(1)}, u32[]{:S(2)}, u32[]{:S(2)}) collective-permute-start(bf16[16,8,384]{2,1,0:T(8,128)(2,1)S(1)} %constant_dynamic-slice_fusion.5), channel_id=1, source_target_pairs={{0,1},{1,0},{2,3},{3,2},{4,5},{5,4},{6,7},{7,6},{8,9},{9,8},{10,11... | collective-permute-start | bytes 294920 | tf_op jit(solution)/shard_map/ppermute | solution.py:378
  12.9 38.4 %collective-permute-start.4 = (bf16[3,8,384]{2,1,0:T(8,128)(2,1)}, bf16[3,8,384]{2,1,0:T(8,128)(2,1)}, u32[]{:S(2)}, u32[]{:S(2)}) collective-permute-start(bf16[3,8,384]{2,1,0:T(8,128)(2,1)} %get-tuple-element.18), channel_id=1, source_target_pairs={{0,3},{1,2},{2,5},{3,4},{4,7},{5,6},{6,9},{7,8},{8,11},{9,10},{10,... | collective-permute-start | bytes 55304 | tf_op jit(solution)/shard_map/ppermute | solution.py:381
  16.9 34.4 %collective-permute-start.3 = (bf16[3,128,384]{2,1,0:T(8,128)(2,1)}, bf16[3,128,384]{2,1,0:T(8,128)(2,1)}, u32[]{:S(2)}, u32[]{:S(2)}) collective-permute-start(bf16[3,128,384]{2,1,0:T(8,128)(2,1)} %get-tuple-element.20), channel_id=1, source_target_pairs={{0,2},{2,4},{4,6},{6,8},{8,10},{10,12},{12,14},{1,3},{3,5},{5,7},{... | collective-permute-start | bytes 884744 | tf_op jit(solution)/shard_map/ppermute | solution.py:379
  21.2 42.5 %collective-permute-start.7 = (bf16[3,8,384]{2,1,0:T(8,128)(2,1)}, bf16[3,8,384]{2,1,0:T(8,128)(2,1)S(1)}, u32[]{:S(2)}, u32[]{:S(2)}) collective-permute-start(bf16[3,8,384]{2,1,0:T(8,128)(2,1)} %get-tuple-element.17), channel_id=1, source_target_pairs={{2,1},{3,0},{4,3},{5,2},{6,5},{7,4},{8,7},{9,6},{10,9},{11,8},{12,... | collective-permute-start | bytes 55304 | tf_op jit(solution)/shard_map/ppermute | solution.py:382
  24.0 41.4 %collective-permute-start.6 = (bf16[3,128,384]{2,1,0:T(8,128)(2,1)}, bf16[3,128,384]{2,1,0:T(8,128)(2,1)S(1)}, u32[]{:S(2)}, u32[]{:S(2)}) collective-permute-start(bf16[3,128,384]{2,1,0:T(8,128)(2,1)} %get-tuple-element.19), channel_id=1, source_target_pairs={{2,0},{4,2},{6,4},{8,6},{10,8},{12,10},{14,12},{3,1},{5,3},{7,5},{... | collective-permute-start | bytes 884744 | tf_op jit(solution)/shard_map/ppermute | solution.py:380
  28.3 36.9 %collective-permute-start.2 = (s32[3,9,128]{2,1,0:T(8,128)S(1)}, s32[3,9,128]{2,1,0:T(8,128)S(1)}, u32[]{:S(2)}, u32[]{:S(2)}) collective-permute-start(s32[3,9,128]{2,1,0:T(8,128)S(1)} %get-tuple-element.25), channel_id=1, source_target_pairs={{0,1},{1,0},{2,3},{3,2},{4,5},{5,4},{6,7},{7,6},{8,9},{9,8},{10,11... | collective-permute-start | bytes 41480 | tf_op jit(solution)/shard_map/ppermute | solution.py:415
  28.5 1.0 copy-start.3
  29.5 1.0 copy-start.5
  30.4 1.0 copy-start.7
  40.9 11.9 %copy-start.4 = (bf16[384,384]{1,0:T(8,128)(2,1)S(1)}, bf16[384,384]{1,0:T(8,128)(2,1)}, u32[]{:S(2)}) copy-start(bf16[384,384]{1,0:T(8,128)(2,1)} %wk_ref.7) | copy-start | bytes 884740
  40.9 11.9 %copy-start.14 = (f32[64,240]{1,0:T(8,128)S(1)}, f32[64,240]{1,0:T(8,128)}, u32[]{:S(2)}) copy-start(f32[64,240]{1,0:T(8,128)} %constant.73.clone.inside_ref) | copy-start | bytes 184324
  51.2 15.5 %copy-start.6 = (bf16[384,384]{1,0:T(8,128)(2,1)S(1)}, bf16[384,384]{1,0:T(8,128)(2,1)}, u32[]{:S(2)}) copy-start(bf16[384,384]{1,0:T(8,128)(2,1)} %wv_ref.7) | copy-start | bytes 884740
  51.2 15.5 %copy-start.8 = (bf16[384,384]{1,0:T(8,128)(2,1)S(1)}, bf16[384,384]{1,0:T(8,128)(2,1)}, u32[]{:S(2)}) copy-start(bf16[384,384]{1,0:T(8,128)(2,1)} %wo_ref.7) | copy-start | bytes 884740
  51.2 27.6 %collective-permute-start.13 = (bf16[512,384]{1,0:T(8,128)(2,1)S(1)}, bf16[512,384]{1,0:T(8,128)(2,1)}, u32[]{:S(2)}, u32[]{:S(2)}) collective-permute-start(bf16[512,384]{1,0:T(8,128)(2,1)S(1)} %shard_map.300.refs_10_), channel_id=1, source_target_pairs={{0,2},{2,0},{4,6},{6,4},{8,10},{10,8},{12,14},{14,12},{1,3},{3,1},... | collective-permute-start | bytes 1179656 | tf_op jit(solution)/shard_map/ppermute | solution.py:401
  51.3 29.0 %collective-permute-start.14 = (bf16[512,384]{1,0:T(8,128)(2,1)}, bf16[512,384]{1,0:T(8,128)(2,1)}, u32[]{:S(2)}, u32[]{:S(2)}) collective-permute-start(bf16[512,384]{1,0:T(8,128)(2,1)} %shard_map.301.refs_11_), channel_id=1, source_target_pairs={{0,2},{2,0},{4,6},{6,4},{8,10},{10,8},{12,14},{14,12},{1,3},{3,1},... | collective-permute-start | bytes 1179656 | tf_op jit(solution)/shard_map/ppermute | solution.py:401
  64.2 16.7 %collective-permute-start.10 = (bf16[512,384]{1,0:T(8,128)(2,1)}, bf16[512,384]{1,0:T(8,128)(2,1)}, u32[]{:S(2)}, u32[]{:S(2)}) collective-permute-start(bf16[512,384]{1,0:T(8,128)(2,1)} %shard_map.301.refs_11_), channel_id=1, source_target_pairs={{0,1},{1,0},{2,3},{3,2},{4,5},{5,4},{6,7},{7,6},{8,9},{9,8},{10,11... | collective-permute-start | bytes 1179656 | tf_op jit(solution)/shard_map/ppermute | solution.py:404
  65.3 16.5 %collective-permute-start.9 = (bf16[512,384]{1,0:T(8,128)(2,1)S(1)}, bf16[512,384]{1,0:T(8,128)(2,1)}, u32[]{:S(2)}, u32[]{:S(2)}) collective-permute-start(bf16[512,384]{1,0:T(8,128)(2,1)S(1)} %shard_map.300.refs_10_), channel_id=1, source_target_pairs={{0,1},{1,0},{2,3},{3,2},{4,5},{5,4},{6,7},{7,6},{8,9},{9,8},{10,11... | collective-permute-start | bytes 1179656 | tf_op jit(solution)/shard_map/ppermute | solution.py:404
  66.6 17.6 %collective-permute-start.12 = (bf16[512,384]{1,0:T(8,128)(2,1)}, bf16[512,384]{1,0:T(8,128)(2,1)}, u32[]{:S(2)}, u32[]{:S(2)}) collective-permute-start(bf16[512,384]{1,0:T(8,128)(2,1)} %shard_map.299.refs_9_), channel_id=1, source_target_pairs={{0,2},{2,0},{4,6},{6,4},{8,10},{10,8},{12,14},{14,12},{1,3},{3,1},... | collective-permute-start | bytes 1179656 | tf_op jit(solution)/shard_map/ppermute | solution.py:401
  66.7 0.8 copy-start.15
  67.5 1.0 copy-start.20
  69.2 18.4 %copy-start.27 = (bf16[16,128,384]{2,1,0:T(8,128)(2,1)S(1)}, bf16[16,128,384]{2,1,0:T(8,128)(2,1)}, u32[]{:S(2)}) copy-start(bf16[16,128,384]{2,1,0:T(8,128)(2,1)} %refs_3_.1) | copy-start | bytes 4718596
  78.8 26.4 %copy-start.34 = (f32[384]{0:T(512)S(1)}, f32[384]{0:T(512)}, u32[]{:S(2)}) copy-start(f32[384]{0:T(512)} %param.44) | copy-start | bytes 4612
  78.8 26.4 %copy-start.35 = (f32[384]{0:T(512)S(1)}, f32[384]{0:T(512)}, u32[]{:S(2)}) copy-start(f32[384]{0:T(512)} %param.49) | copy-start | bytes 4612
  78.8 27.0 %copy-start.36 = (f32[384]{0:T(512)S(1)}, f32[384]{0:T(512)}, u32[]{:S(2)}) copy-start(f32[384]{0:T(512)} %param.43) | copy-start | bytes 4612
  78.8 10.9 %collective-permute-start.15 = (bf16[512,384]{1,0:T(8,128)(2,1)S(1)}, bf16[512,384]{1,0:T(8,128)(2,1)S(1)}, u32[]{:S(2)}, u32[]{:S(2)}) collective-permute-start(bf16[512,384]{1,0:T(8,128)(2,1)S(1)} %shard_map.302.refs_12_), channel_id=1, source_target_pairs={{0,2},{2,0},{4,6},{6,4},{8,10},{10,8},{12,14},{14,12},{1,3},{3,1},... | collective-permute-start | bytes 1179656 | tf_op jit(solution)/shard_map/ppermute | solution.py:401
  80.3 10.1 %collective-permute-start.8 = (bf16[512,384]{1,0:T(8,128)(2,1)}, bf16[512,384]{1,0:T(8,128)(2,1)S(1)}, u32[]{:S(2)}, u32[]{:S(2)}) collective-permute-start(bf16[512,384]{1,0:T(8,128)(2,1)} %shard_map.299.refs_9_), channel_id=1, source_target_pairs={{0,1},{1,0},{2,3},{3,2},{4,5},{5,4},{6,7},{7,6},{8,9},{9,8},{10,11... | collective-permute-start | bytes 1179656 | tf_op jit(solution)/shard_map/ppermute | solution.py:404
  80.9 9.5 %collective-permute-start.11 = (bf16[512,384]{1,0:T(8,128)(2,1)S(1)}, bf16[512,384]{1,0:T(8,128)(2,1)S(1)}, u32[]{:S(2)}, u32[]{:S(2)}) collective-permute-start(bf16[512,384]{1,0:T(8,128)(2,1)S(1)} %shard_map.302.refs_12_), channel_id=1, source_target_pairs={{0,1},{1,0},{2,3},{3,2},{4,5},{5,4},{6,7},{7,6},{8,9},{9,8},{10,11... | collective-permute-start | bytes 1179656 | tf_op jit(solution)/shard_map/ppermute | solution.py:404
  81.0 0.8 copy-start.10
  81.8 12.4 %collective-permute-start.21 = (bf16[512,384]{1,0:T(8,128)(2,1)}, bf16[512,384]{1,0:T(8,128)(2,1)}, u32[]{:S(2)}, u32[]{:S(2)}) collective-permute-start(bf16[512,384]{1,0:T(8,128)(2,1)} %collective-permute-done.13.refs_18_), channel_id=1, source_target_pairs={{0,4},{4,8},{6,2},{8,12},{10,6},{14,10},{1,5},{5,9},{7,3},{9,13},{... | collective-permute-start | bytes 1179656 | tf_op jit(solution)/shard_map/ppermute | solution.py:402
  84.3 18.4 %collective-permute-start.22 = (bf16[512,384]{1,0:T(8,128)(2,1)}, bf16[512,384]{1,0:T(8,128)(2,1)}, u32[]{:S(2)}, u32[]{:S(2)}) collective-permute-start(bf16[512,384]{1,0:T(8,128)(2,1)} %collective-permute-done.14.refs_19_), channel_id=1, source_target_pairs={{0,4},{4,8},{6,2},{8,12},{10,6},{14,10},{1,5},{5,9},{7,3},{9,13},{... | collective-permute-start | bytes 1179656 | tf_op jit(solution)/shard_map/ppermute | solution.py:402
  89.7 18.0 %collective-permute-start.17 = (bf16[512,384]{1,0:T(8,128)(2,1)}, bf16[512,384]{1,0:T(8,128)(2,1)S(1)}, u32[]{:S(2)}, u32[]{:S(2)}) collective-permute-start(bf16[512,384]{1,0:T(8,128)(2,1)} %collective-permute-done.13.refs_18_), channel_id=1, source_target_pairs={{0,1},{1,0},{2,3},{3,2},{4,5},{5,4},{6,7},{7,6},{8,9},{9,8},{10,11... | collective-permute-start | bytes 1179656 | tf_op jit(solution)/shard_map/ppermute | solution.py:404
  90.4 19.8 %collective-permute-start.18 = (bf16[512,384]{1,0:T(8,128)(2,1)}, bf16[512,384]{1,0:T(8,128)(2,1)S(1)}, u32[]{:S(2)}, u32[]{:S(2)}) collective-permute-start(bf16[512,384]{1,0:T(8,128)(2,1)} %collective-permute-done.14.refs_19_), channel_id=1, source_target_pairs={{0,1},{1,0},{2,3},{3,2},{4,5},{5,4},{6,7},{7,6},{8,9},{9,8},{10,11... | collective-permute-start | bytes 1179656 | tf_op jit(solution)/shard_map/ppermute | solution.py:404
  90.4 20.6 %collective-permute-start.20 = (bf16[512,384]{1,0:T(8,128)(2,1)}, bf16[512,384]{1,0:T(8,128)(2,1)}, u32[]{:S(2)}, u32[]{:S(2)}) collective-permute-start(bf16[512,384]{1,0:T(8,128)(2,1)} %collective-permute-done.12.refs_17_), channel_id=1, source_target_pairs={{0,4},{4,8},{6,2},{8,12},{10,6},{14,10},{1,5},{5,9},{7,3},{9,13},{... | collective-permute-start | bytes 1179656 | tf_op jit(solution)/shard_map/ppermute | solution.py:402
  94.2 26.6 %collective-permute-start.16 = (bf16[512,384]{1,0:T(8,128)(2,1)}, bf16[512,384]{1,0:T(8,128)(2,1)S(1)}, u32[]{:S(2)}, u32[]{:S(2)}) collective-permute-start(bf16[512,384]{1,0:T(8,128)(2,1)} %collective-permute-done.12.refs_17_), channel_id=1, source_target_pairs={{0,1},{1,0},{2,3},{3,2},{4,5},{5,4},{6,7},{7,6},{8,9},{9,8},{10,11... | collective-permute-start | bytes 1179656 | tf_op jit(solution)/shard_map/ppermute | solution.py:404
  102.6 16.9 %collective-permute-start.23 = (bf16[512,384]{1,0:T(8,128)(2,1)S(1)}, bf16[512,384]{1,0:T(8,128)(2,1)}, u32[]{:S(2)}, u32[]{:S(2)}) collective-permute-start(bf16[512,384]{1,0:T(8,128)(2,1)S(1)} %collective-permute-done.15.refs_20_), channel_id=1, source_target_pairs={{0,4},{4,8},{6,2},{8,12},{10,6},{14,10},{1,5},{5,9},{7,3},{9,13},{... | collective-permute-start | bytes 1179656 | tf_op jit(solution)/shard_map/ppermute | solution.py:402
  107.7 13.1 %copy-start.28 = (bf16[512,384]{1,0:T(8,128)(2,1)}, bf16[512,384]{1,0:T(8,128)(2,1)S(1)}, u32[]{:S(2)}) copy-start(bf16[512,384]{1,0:T(8,128)(2,1)S(1)} %collective-permute-done.17.refs_22_) | copy-start | bytes 1179652
  107.7 19.0 %collective-permute-start.19 = (bf16[512,384]{1,0:T(8,128)(2,1)S(1)}, bf16[512,384]{1,0:T(8,128)(2,1)}, u32[]{:S(2)}, u32[]{:S(2)}) collective-permute-start(bf16[512,384]{1,0:T(8,128)(2,1)S(1)} %collective-permute-done.15.refs_20_), channel_id=1, source_target_pairs={{0,1},{1,0},{2,3},{3,2},{4,5},{5,4},{6,7},{7,6},{8,9},{9,8},{10,11... | collective-permute-start | bytes 1179656 | tf_op jit(solution)/shard_map/ppermute | solution.py:404
  110.2 10.6 %copy-start.29 = (bf16[512,384]{1,0:T(8,128)(2,1)}, bf16[512,384]{1,0:T(8,128)(2,1)S(1)}, u32[]{:S(2)}) copy-start(bf16[512,384]{1,0:T(8,128)(2,1)S(1)} %collective-permute-done.18.refs_23_) | copy-start | bytes 1179652
  110.2 16.5 %collective-permute-start.25 = (bf16[512,384]{1,0:T(8,128)(2,1)}, bf16[512,384]{1,0:T(8,128)(2,1)}, u32[]{:S(2)}, u32[]{:S(2)}) collective-permute-start(bf16[512,384]{1,0:T(8,128)(2,1)} %collective-permute-done.21.refs_26_), channel_id=1, source_target_pairs={{0,1},{1,0},{2,3},{3,2},{4,5},{5,4},{6,7},{7,6},{8,9},{9,8},{10,11... | collective-permute-start | bytes 1179656 | tf_op jit(solution)/shard_map/ppermute | solution.py:404
  111.0 15.7 %collective-permute-start.26 = (bf16[512,384]{1,0:T(8,128)(2,1)}, bf16[512,384]{1,0:T(8,128)(2,1)}, u32[]{:S(2)}, u32[]{:S(2)}) collective-permute-start(bf16[512,384]{1,0:T(8,128)(2,1)} %collective-permute-done.22.refs_27_), channel_id=1, source_target_pairs={{0,1},{1,0},{2,3},{3,2},{4,5},{5,4},{6,7},{7,6},{8,9},{9,8},{10,11... | collective-permute-start | bytes 1179656 | tf_op jit(solution)/shard_map/ppermute | solution.py:404
  119.5 7.2 %collective-permute-start.24 = (bf16[512,384]{1,0:T(8,128)(2,1)}, bf16[512,384]{1,0:T(8,128)(2,1)}, u32[]{:S(2)}, u32[]{:S(2)}) collective-permute-start(bf16[512,384]{1,0:T(8,128)(2,1)} %collective-permute-done.20.refs_25_), channel_id=1, source_target_pairs={{0,1},{1,0},{2,3},{3,2},{4,5},{5,4},{6,7},{7,6},{8,9},{9,8},{10,11... | collective-permute-start | bytes 1179656 | tf_op jit(solution)/shard_map/ppermute | solution.py:404
  120.8 6.0 %collective-permute-start.27 = (bf16[512,384]{1,0:T(8,128)(2,1)}, bf16[512,384]{1,0:T(8,128)(2,1)}, u32[]{:S(2)}, u32[]{:S(2)}) collective-permute-start(bf16[512,384]{1,0:T(8,128)(2,1)} %collective-permute-done.23.refs_28_), channel_id=1, source_target_pairs={{0,1},{1,0},{2,3},{3,2},{4,5},{5,4},{6,7},{7,6},{8,9},{9,8},{10,11... | collective-permute-start | bytes 1179656 | tf_op jit(solution)/shard_map/ppermute | solution.py:404
  120.8 2.3 %copy-start.30 = (s32[3,1,9,128]{3,2,1,0:T(8,128)S(1)}, s32[3,1,9,128]{3,2,1,0:T(8,128)}, u32[]{:S(2)}) copy-start(s32[3,1,9,128]{3,2,1,0:T(8,128)} %get-tuple-element.24) | copy-start | bytes 41476
  120.8 2.3 %copy-start.32 = (s32[3,9,128]{2,1,0:T(8,128)S(1)}, s32[3,9,128]{2,1,0:T(8,128)}, u32[]{:S(2)}) copy-start(s32[3,9,128]{2,1,0:T(8,128)} %copy-done.31) | copy-start | bytes 41476
  120.8 5.9 %copy-start.11 = (bf16[512,384]{1,0:T(8,128)(2,1)S(1)}, bf16[512,384]{1,0:T(8,128)(2,1)}, u32[]{:S(2)}) copy-start(bf16[512,384]{1,0:T(8,128)(2,1)} %copy-done.10) | copy-start | bytes 1179652
  120.8 5.9 %copy-start.16 = (bf16[384,384]{1,0:T(8,128)(2,1)S(1)}, bf16[384,384]{1,0:T(8,128)(2,1)}, u32[]{:S(2)}) copy-start(bf16[384,384]{1,0:T(8,128)(2,1)} %refs_6_.1) | copy-start | bytes 884740
  120.8 5.9 %copy-start.17 = (bf16[384,384]{1,0:T(8,128)(2,1)S(1)}, bf16[384,384]{1,0:T(8,128)(2,1)}, u32[]{:S(2)}) copy-start(bf16[384,384]{1,0:T(8,128)(2,1)} %refs_7_.1) | copy-start | bytes 884740
  126.8 1.0 copy-start.18
  169.5 16.2 %collective-permute-start.28 = (bf16[2,128,384]{2,1,0:T(8,128)(2,1)S(1)}, bf16[2,128,384]{2,1,0:T(8,128)(2,1)S(1)}, u32[]{:S(2)}, u32[]{:S(2)}) collective-permute-start(bf16[2,128,384]{2,1,0:T(8,128)(2,1)S(1)} %get-tuple-element.16), channel_id=1, source_target_pairs={{0,2},{2,4},{4,6},{6,8},{8,10},{10,12},{12,14},{1,3},{3,5},{5,7},{... | collective-permute-start | bytes 589832 | tf_op jit(solution)/shard_map/ppermute | solution.py:379
  171.4 14.3 %collective-permute-start.29 = (bf16[2,128,384]{2,1,0:T(8,128)(2,1)S(1)}, bf16[2,128,384]{2,1,0:T(8,128)(2,1)S(1)}, u32[]{:S(2)}, u32[]{:S(2)}) collective-permute-start(bf16[2,128,384]{2,1,0:T(8,128)(2,1)S(1)} %get-tuple-element.15), channel_id=1, source_target_pairs={{2,0},{4,2},{6,4},{8,6},{10,8},{12,10},{14,12},{3,1},{5,3},{7,5},{... | collective-permute-start | bytes 589832 | tf_op jit(solution)/shard_map/ppermute | solution.py:380
  176.6 9.1 %collective-permute-start.30 = (bf16[16,8,384]{2,1,0:T(8,128)(2,1)S(1)}, bf16[16,8,384]{2,1,0:T(8,128)(2,1)S(1)}, u32[]{:S(2)}, u32[]{:S(2)}) collective-permute-start(bf16[16,8,384]{2,1,0:T(8,128)(2,1)S(1)} %constant_dynamic-slice_fusion.4), channel_id=1, source_target_pairs={{0,1},{1,0},{2,3},{3,2},{4,5},{5,4},{6,7},{7,6},{8,9},{9,8},{10,11... | collective-permute-start | bytes 294920 | tf_op jit(solution)/shard_map/ppermute | solution.py:378
  178.4 6.5 %collective-permute-start.31 = (bf16[2,8,384]{2,1,0:T(8,128)(2,1)S(1)}, bf16[2,8,384]{2,1,0:T(8,128)(2,1)S(1)}, u32[]{:S(2)}, u32[]{:S(2)}) collective-permute-start(bf16[2,8,384]{2,1,0:T(8,128)(2,1)S(1)} %get-tuple-element.14), channel_id=1, source_target_pairs={{0,3},{1,2},{2,5},{3,4},{4,7},{5,6},{6,9},{7,8},{8,11},{9,10},{10,... | collective-permute-start | bytes 36872 | tf_op jit(solution)/shard_map/ppermute | solution.py:381
  180.4 5.4 %collective-permute-start.32 = (bf16[2,8,384]{2,1,0:T(8,128)(2,1)S(1)}, bf16[2,8,384]{2,1,0:T(8,128)(2,1)S(1)}, u32[]{:S(2)}, u32[]{:S(2)}) collective-permute-start(bf16[2,8,384]{2,1,0:T(8,128)(2,1)S(1)} %get-tuple-element.13), channel_id=1, source_target_pairs={{2,1},{3,0},{4,3},{5,2},{6,5},{7,4},{8,7},{9,6},{10,9},{11,8},{12,... | collective-permute-start | bytes 36872 | tf_op jit(solution)/shard_map/ppermute | solution.py:382
  185.7 1.4 copy-start.9
  187.1 1.4 copy-start.12
  (6 other events, 4.2 us)
